TPU v7x, 32 devices: a whole 2x2x4 slice. The times are simulated.
32 devices in a mesh: groups: 2 (over y), tm: 4 (over z), lon: 2 (over x), probe: 2 (over core).
Axes of the slice: x: 2, y: 2, z: 4, core: 2. Of those that a mesh axis runs over, the one named last changes fastest.
Arguments:
- winds: bfloat16 [2, 8, 2, 36, 72, 192], P(None, ('groups', 'tm'), None, None, 'lon'), parts along dimension 1, may hold values from -0.44921875 to 0.44921875
- mixing: float32 [36, 36], replicated, as said below
- obs_cell: int32 [8, 2, 2048], P(('groups', 'tm'), 'lon'), parts along dimension 0, may hold values from 0 to 248831
- obs_weight: float32 [8, 2, 2048], P(('groups', 'tm'), 'lon'), parts along dimension 0, may hold values from 0.5 to 4
- probe_sign: int32 [4, 8, 2, 2048], P('probe', ('groups', 'tm'), 'lon'), parts along dimension 1, may hold values from 0 to 1
- week_map: int32 [8, 2], P(('groups', 'tm')), parts along dimension 0, may hold values from 0 to 1
- prior_precision: float32 [4, 72, 192], P('groups', 'lon', 'tm'), parts along dimension 0, may hold values from 0.1 to 1
Outputs:
- hessian_diag: float32 [2, 4, 72, 192], P('probe', 'groups', 'lon', 'tm'), parts along dimension 1
There are 2 independent parts, one for each index of `groups`. A program takes and returns all parts, laid end to end along the dimension named above; an argument that names none is the same for every part. Nothing has to cross between parts.
Inputs may be any that keep to these rules, and one draw needn't show every extreme that they name: mixing = 0.55 on the diagonal plus 0.45 / 36 times a factor between 0.5 and 1.4 in every entry.
All inputs are finite; a program needn't handle non-finite values.
Results may differ from a plain program's by a relative error of at most 0.0003.
Values may be sent and summed in bfloat16 or wider, within the bound.
A program may use at most 128 MiB of HBM per device.

v0:
```python
import jax
import jax.numpy as jnp
from jax import lax
from jax.sharding import PartitionSpec as P


def with_halo(block, sides, width):
    for axis, dim in sides:
        count = lax.axis_size(axis)
        forward = [(i, i + 1) for i in range(count - 1)]
        forward.append((count - 1, 0))
        backward = [(target, source) for source, target in forward]
        low = lax.ppermute(
            lax.slice_in_dim(block, block.shape[dim] - width, None, axis=dim), axis, forward
        )
        high = lax.ppermute(lax.slice_in_dim(block, 0, width, axis=dim), axis, backward)
        block = jnp.concatenate([low, block, high], axis=dim)
    return block


def passed_along(block, axis, distance):
    devices = range(lax.axis_size(axis))
    route = [(i - distance, i) for i in devices if i - distance in devices]
    return lax.ppermute(block, axis, route)


def adjoint_step(adjoint, east_face, north_face, mixing):
    adjoint = jnp.einsum("lk,...lxy->...kxy", mixing, adjoint, precision=lax.Precision.HIGHEST)
    east_pos = jnp.maximum(east_face, 0.0)
    west_neg = jnp.minimum(jnp.roll(east_face, 1, axis=-2), 0.0)
    adjoint = (
        adjoint
        + east_pos * (jnp.roll(adjoint, -1, axis=-2) - adjoint)
        + west_neg * (adjoint - jnp.roll(adjoint, 1, axis=-2))
    )
    lat_count = north_face.shape[-1]
    row_keep = (jnp.arange(lat_count) < lat_count - 1).astype(north_face.dtype)
    north_cut = north_face * row_keep
    north_pos = jnp.maximum(north_cut, 0.0)
    south_neg = jnp.minimum(
        jnp.concatenate([jnp.zeros_like(north_cut[..., :1]), north_cut[..., :-1]], axis=-1), 0.0
    )
    above_row = jnp.concatenate([adjoint[..., 1:], jnp.zeros_like(adjoint[..., :1])], axis=-1)
    below_row = jnp.concatenate([jnp.zeros_like(adjoint[..., :1]), adjoint[..., :-1]], axis=-1)
    return adjoint + north_pos * (above_row - adjoint) + south_neg * (adjoint - below_row)


def section_pass(adjoint, forcing, wind_ext, onehot, mixing, hours_sec, band_cols):
    flux_part = jnp.zeros(
        adjoint.shape[:-3] + (onehot.shape[1], band_cols, adjoint.shape[-1]), jnp.float32
    )
    for hour_id in reversed(range(hours_sec)):
        if hour_id == 0:
            adjoint = adjoint + forcing
        surface = adjoint[..., 0, hours_sec : hours_sec + band_cols, :]
        flux_part = flux_part + onehot[hour_id][:, None, None] * surface[..., None, :, :]
        east_face = wind_ext[0, hour_id].astype(jnp.float32)
        north_face = wind_ext[1, hour_id].astype(jnp.float32)
        adjoint = adjoint_step(adjoint, east_face, north_face, mixing)
    return (adjoint[..., hours_sec : hours_sec + band_cols, :], flux_part)


def on_device(winds, mixing, obs_cell, obs_weight, probe_sign, week_map, prior_precision):
    hours_sec = winds.shape[2]
    levels = winds.shape[3]
    band_cols = winds.shape[4]
    lat_rows = winds.shape[5]
    probes = probe_sign.shape[0]
    week_count = prior_precision.shape[0]
    sections = lax.axis_size("tm")
    section_id = lax.axis_index("tm")
    ext_cols = band_cols + 2 * hours_sec
    wind_ext = with_halo(winds[:, 0], (("lon", 3),), hours_sec)
    value = (2 * probe_sign[:, 0, 0] - 1).astype(jnp.float32) * obs_weight[0, 0][None]
    packed = obs_cell[0, 0].astype(jnp.float32)
    bundle = jnp.concatenate([packed[None], value], axis=0)[:, None, :]
    bundle = with_halo(bundle, (("lon", 1),), 1)
    cells = bundle[0].astype(jnp.int32)
    level_id = cells // (band_cols * lat_rows)
    remainder = cells % (band_cols * lat_rows)
    offsets = jnp.array([-1, 0, 1], jnp.int32)[:, None] * band_cols
    column = remainder // lat_rows + hours_sec + offsets
    lat_id = remainder % lat_rows
    inside = (column >= 0) & (column < ext_cols)
    limit = levels * ext_cols * lat_rows
    places = (level_id * ext_cols + column) * lat_rows + lat_id
    places = jnp.where(inside, places, limit).reshape(-1)
    forcing = (
        jnp.zeros((probes, limit), jnp.float32)
        .at[:, places]
        .add(bundle[1:].reshape(probes, -1), mode="drop")
    )
    forcing = forcing.reshape(probes, levels, ext_cols, lat_rows)
    onehot = (week_map[0][:, None] == jnp.arange(week_count)[None, :]).astype(jnp.float32)
    flux_sums = jnp.zeros((probes, week_count, band_cols, lat_rows), jnp.float32)

    def sweep(segment_id, state_pair):
        incoming, flux_sums = state_pair
        padded = with_halo(incoming, (("lon", 2),), hours_sec)
        active = section_id == sections - 1 - segment_id

        def working(unused):
            return section_pass(padded, forcing, wind_ext, onehot, mixing, hours_sec, band_cols)

        def waiting(unused):
            return (incoming, jnp.zeros_like(flux_sums))

        outgoing, flux_part = lax.cond(active, working, waiting, None)
        incoming = passed_along(outgoing, "tm", -1)
        return (incoming, flux_sums + flux_part)

    start = jnp.zeros((probes, levels, band_cols, lat_rows), jnp.float32)
    unused_state, flux_sums = lax.fori_loop(0, sections, sweep, (start, flux_sums))
    summed = lax.psum_scatter(flux_sums, "tm", scatter_dimension=3, tiled=True)
    estimate = prior_precision + jnp.mean(summed * summed, axis=0)
    return estimate[None]


def solution(mesh):
    placed = (
        P(None, ("groups", "tm"), None, None, "lon", None),
        P(),
        P(("groups", "tm"), "lon", None),
        P(("groups", "tm"), "lon", None),
        P("probe", ("groups", "tm"), "lon", None),
        P(("groups", "tm"), None),
        P("groups", "lon", "tm"),
    )
    return jax.shard_map(
        on_device,
        mesh=mesh,
        in_specs=placed,
        out_specs=P("probe", "groups", "lon", "tm"),
        check_vma=False,
    )
```

profile of v0, /device:TPU:9, one launch (start us, length us, event | category | flops | bytes accessed | tf_op | source)
XLA Modules:
  0.0 692.5 jit_solution(2790992229335467887)
XLA Ops:
  8.7 1.3 collective-permute-start.5
  10.3 2.3 copy.44
  12.6 1.6 copy-done.7
  17.3 207.5 %scatter_fusion = f32[2,276480]{1,0:T(2,128)S(1)} fusion(f32[2,276480]{1,0:T(2,128)S(1)} %broadcast_in_dim.13, s32[6144]{0:T(1024)S(1)} %bitcast.83, f32[6144,2]{0,1:T(2,128)S(1)} %bitcast.78), kind=kCustom, calls=%fused_computation | custom fusion | flops 12288 | bytes 172032 | tf_op jit(solution)/shard_map/scatter-add | solution.py:91
  224.7 3.8 reshape.239
  228.5 4.6 copy.29
  233.1 2.1 pad_maximum_fusion.1
  235.8 421.8 %while.19 = (s32[]{:T(128)}, f32[2,36,36,192]{3,0,2,1:T(2,128)S(1)}, f32[2,2,36,192]{3,2,1,0:T(8,128)}, s32[]{:T(128)}, f32[36,36]{0,1:T(8,128)S(1)}, /*index=5*...) while((s32[]{:T(128)}, ...), condition=%wide.region_4.5_spmd.clone, body=%wide.region_1.4_spmd.clone.sunk | while | flops 499682688 | bytes 189307088 | solution.py:113
  236.0 2.5 copy.47
  241.7 2.1 collective-permute-done
  243.8 3.2 collective-permute-done.1
  247.0 2.1 pad_maximum_fusion.5
  249.8 5.5 copy.48
  255.2 2.2 collective-permute-start.2
  258.4 55.3 %collective-permute-done.2 = f32[2,36,36,192]{3,0,2,1:T(2,128)S(1)} collective-permute-done((f32[2,36,36,192]{3,0,2,1:T(2,128)}, f32[2,36,36,192]{3,0,2,1:T(2,128)S(1)}, u32[]{:S(2)}, u32[]{:S(2)}) %collective-permute-start.2) | collective-permute-done | bytes 1990688 | tf_op jit(solution)/shard_map/while/body/eval_jaxpr/ppermute | solution.py:24
  313.7 2.5 copy.47
  319.4 2.1 collective-permute-done
  321.4 1.8 collective-permute-done.1
  323.2 2.1 pad_maximum_fusion.5
  325.9 5.5 copy.48
  331.4 2.4 collective-permute-start.2
  334.9 117.0 %collective-permute-done.2 = f32[2,36,36,192]{3,0,2,1:T(2,128)S(1)} collective-permute-done((f32[2,36,36,192]{3,0,2,1:T(2,128)}, f32[2,36,36,192]{3,0,2,1:T(2,128)S(1)}, u32[]{:S(2)}, u32[]{:S(2)}) %collective-permute-start.2) | collective-permute-done | bytes 1990688 | tf_op jit(solution)/shard_map/while/body/eval_jaxpr/ppermute | solution.py:24
  451.8 2.5 copy.47
  455.3 1.3 collective-permute-start
  457.5 2.1 collective-permute-done
  459.6 1.8 collective-permute-done.1
  461.3 2.1 pad_maximum_fusion.5
  463.4 32.8 %conditional.3 = (f32[2,36,36,192]{3,1,2,0:T(8,128)}, f32[2,2,36,192]{3,2,1,0:T(8,128)}) conditional(s32[]{:T(128)} %convert_element_type.115, f32[2,36,36,192]{3,1,2,0:T(8,128)} %copy.47, (f32[2,36,40,192]{3,1,2,0:T(8,128)S(1)}, f32[36,36]{0,1:T(8,128)S(1)}, bf16[2,2,36,40,192]{4,2,3,1,0:T(8,128)(2,1)S(1)}, f32[2,36,40,192]{3,1,2,0:T(8,128)}, ...), branch_computations={%region_2.2_spmd, %region_3.3_spmd} | conditional | flops 498521472 | bytes 157566688 | solution.py:108
  463.4 1.5 bitcast_convert_fusion
  465.4 2.5 broadcast_maximum_fusion
  467.9 3.1 convolution_bitcast_fusion.1
  472.9 2.8 fusion.21
  475.7 1.7 pad_minimum_fusion.1
  477.4 4.8 add_add_fusion
  482.2 3.1 convolution_bitcast_fusion
  492.0 3.0 fusion.11
  496.2 5.5 copy.48
  501.7 1.9 collective-permute-start.2
  504.6 51.9 %collective-permute-done.2 = f32[2,36,36,192]{3,0,2,1:T(2,128)S(1)} collective-permute-done((f32[2,36,36,192]{3,0,2,1:T(2,128)}, f32[2,36,36,192]{3,0,2,1:T(2,128)S(1)}, u32[]{:S(2)}, u32[]{:S(2)}) %collective-permute-start.2) | collective-permute-done | bytes 1990688 | tf_op jit(solution)/shard_map/while/body/eval_jaxpr/ppermute | solution.py:24
  556.5 2.5 copy.47
  560.0 1.3 collective-permute-start
  562.2 2.1 collective-permute-done
  564.3 1.8 collective-permute-done.1
  566.0 2.1 pad_maximum_fusion.5
  568.8 5.5 copy.48
  574.2 34.3 %collective-permute-start.2 = (f32[2,36,36,192]{3,0,2,1:T(2,128)}, f32[2,36,36,192]{3,0,2,1:T(2,128)S(1)}, u32[]{:S(2)}, u32[]{:S(2)}) collective-permute-start(f32[2,36,36,192]{3,0,2,1:T(2,128)} %copy.48), channel_id=1, source_target_pairs={{4,0},{8,4},{12,8},{5,1},{9,5},{13,9},{6,2},{10,6},{14,10},{7,3},{... | collective-permute-start | bytes 5971976 | tf_op jit(solution)/shard_map/while/body/eval_jaxpr/ppermute | solution.py:24
  609.5 48.1 %collective-permute-done.2 = f32[2,36,36,192]{3,0,2,1:T(2,128)S(1)} collective-permute-done((f32[2,36,36,192]{3,0,2,1:T(2,128)}, f32[2,36,36,192]{3,0,2,1:T(2,128)S(1)}, u32[]{:S(2)}, u32[]{:S(2)}) %collective-permute-start.2) | collective-permute-done | bytes 1990688 | tf_op jit(solution)/shard_map/while/body/eval_jaxpr/ppermute | solution.py:24
  659.8 23.3 %reduce-scatter.4.cloned.1.call-done = f32[48,144]{1,0:T(8,128)} async-done(((f32[192,144]{1,0:T(8,128)}), f32[48,144]{1,0:T(8,128)}) %reduce-scatter.4.cloned.1.call-update) | async-done | bytes 27664
  (134 shorter events, 39.0 us)
Async XLA Ops:
  6.5 676.6 %reduce-scatter.4.cloned.1.call-start = ((), (), s32[]{:S(2)}) async-start(), calls=%async_computation.1 | async-start | bytes 245760
  7.3 8.5 %copy-start.13 = (s32[3]{0:T(128)S(1)}, s32[3]{0:T(128)}, u32[]{:S(2)}) copy-start(s32[3]{0:T(128)} %constant.105) | copy-start | bytes 40
  8.7 7.2 %copy-start.12 = (f32[36,36]{1,0:T(8,128)S(1)}, f32[36,36]{1,0:T(8,128)}, u32[]{:S(2)}) copy-start(f32[36,36]{1,0:T(8,128)} %param.13) | copy-start | bytes 15556
  8.7 7.2 %collective-permute-start.5 = (f32[3,1,2048]{2,0,1:T(4,128)S(1)}, f32[3,1,2048]{2,0,1:T(4,128)S(1)}, u32[]{:S(2)}, u32[]{:S(2)}) collective-permute-start(f32[3,1,2048]{2,0,1:T(4,128)S(1)} %maximum_bitcast_fusion), channel_id=1, source_target_pairs={{0,2},{2,0},{1,3},{3,1},{4,6},{6,4},{5,7},{7,5},{8,10},{10,8},{9,1... | collective-permute-start | bytes 73736 | tf_op jit(solution)/shard_map/ppermute | solution.py:13
  10.0 5.9 collective-permute-start.6
  12.6 1.6 copy-start.7
  14.2 218.8 %collective-permute-start.3 = (bf16[2,2,36,2,192]{4,2,3,1,0:T(8,128)(2,1)S(1)}, bf16[2,2,36,2,192]{4,2,3,1,0:T(8,128)(2,1)S(1)}, u32[]{:S(2)}, u32[]{:S(2)}) collective-permute-start(bf16[2,2,36,2,192]{4,2,3,1,0:T(8,128)(2,1)S(1)} %get-tuple-element.283), channel_id=1, source_target_pairs={{0,2},{2,0},{1,3},{3,1},{4,6},{6,4},{5,7},{7,5},{8,10},{10,8},{9,1... | collective-permute-start | bytes 331784 | tf_op jit(solution)/shard_map/ppermute | solution.py:13
  15.5 217.6 %collective-permute-start.4 = (bf16[2,2,36,2,192]{4,2,3,1,0:T(8,128)(2,1)S(1)}, bf16[2,2,36,2,192]{4,2,3,1,0:T(8,128)(2,1)S(1)}, u32[]{:S(2)}, u32[]{:S(2)}) collective-permute-start(bf16[2,2,36,2,192]{4,2,3,1,0:T(8,128)(2,1)S(1)} %get-tuple-element.284), channel_id=1, source_target_pairs={{2,0},{0,2},{3,1},{1,3},{6,4},{4,6},{7,5},{5,7},{10,8},{8,10},{11,... | collective-permute-start | bytes 331784 | tf_op jit(solution)/shard_map/ppermute | solution.py:16
  228.5 4.6 copy-start.8
  233.1 2.8 copy-start.14
  239.6 4.2 collective-permute-start
  240.7 6.3 collective-permute-start.1
  241.7 7.4 %copy-start.2 = (bf16[2,2,36,40,192]{4,2,3,1,0:T(8,128)(2,1)S(1)}, bf16[2,2,36,40,192]{4,2,3,1,0:T(8,128)(2,1)}, u32[]{:S(2)}) copy-start(bf16[2,2,36,40,192]{4,2,3,1,0:T(8,128)(2,1)} %get-tuple-element.373) | copy-start | bytes 6635524 | tf_op jit(solution)/shard_map/while
  249.8 7.6 %copy-start.9 = (f32[2,2,36,192]{3,2,1,0:T(8,128)S(1)}, f32[2,2,36,192]{3,2,1,0:T(8,128)}, u32[]{:S(2)}) copy-start(f32[2,2,36,192]{3,2,1,0:T(8,128)} %get-tuple-element.359) | copy-start | bytes 331780 | tf_op jit(solution)/shard_map/while
  249.8 63.9 %copy-start.15 = (s32[1,2]{1,0:T(1,128)S(1)}, s32[1,2]{1,0:T(1,128)}, u32[]{:S(2)}) copy-start(s32[1,2]{1,0:T(1,128)} %get-tuple-element.407) | copy-start | bytes 28 | tf_op jit(solution)/shard_map/while
  255.2 58.4 %collective-permute-start.2 = (f32[2,36,36,192]{3,0,2,1:T(2,128)}, f32[2,36,36,192]{3,0,2,1:T(2,128)S(1)}, u32[]{:S(2)}, u32[]{:S(2)}) collective-permute-start(f32[2,36,36,192]{3,0,2,1:T(2,128)} %copy.48), channel_id=1, source_target_pairs={{4,0},{8,4},{12,8},{5,1},{9,5},{13,9},{6,2},{10,6},{14,10},{7,3},{... | collective-permute-start | bytes 5971976 | tf_op jit(solution)/shard_map/while/body/eval_jaxpr/ppermute | solution.py:24
  258.4 55.3 %copy-start.10 = (f32[2,2,36,192]{3,2,1,0:T(8,128)}, f32[2,2,36,192]{3,2,1,0:T(8,128)S(1)}, u32[]{:S(2)}) copy-start(f32[2,2,36,192]{3,2,1,0:T(8,128)S(1)} %select_add_fusion.2) | copy-start | bytes 331780 | tf_op jit(solution)/shard_map/while
  317.2 4.2 collective-permute-start
  318.4 4.8 collective-permute-start.1
  319.4 5.9 copy-start.2
  325.9 7.9 %copy-start.9 = (f32[2,2,36,192]{3,2,1,0:T(8,128)S(1)}, f32[2,2,36,192]{3,2,1,0:T(8,128)}, u32[]{:S(2)}) copy-start(f32[2,2,36,192]{3,2,1,0:T(8,128)} %get-tuple-element.359) | copy-start | bytes 331780 | tf_op jit(solution)/shard_map/while
  325.9 125.9 %copy-start.15 = (s32[1,2]{1,0:T(1,128)S(1)}, s32[1,2]{1,0:T(1,128)}, u32[]{:S(2)}) copy-start(s32[1,2]{1,0:T(1,128)} %get-tuple-element.407) | copy-start | bytes 28 | tf_op jit(solution)/shard_map/while
  331.4 120.4 %collective-permute-start.2 = (f32[2,36,36,192]{3,0,2,1:T(2,128)}, f32[2,36,36,192]{3,0,2,1:T(2,128)S(1)}, u32[]{:S(2)}, u32[]{:S(2)}) collective-permute-start(f32[2,36,36,192]{3,0,2,1:T(2,128)} %copy.48), channel_id=1, source_target_pairs={{4,0},{8,4},{12,8},{5,1},{9,5},{13,9},{6,2},{10,6},{14,10},{7,3},{... | collective-permute-start | bytes 5971976 | tf_op jit(solution)/shard_map/while/body/eval_jaxpr/ppermute | solution.py:24
  334.8 117.0 %copy-start.10 = (f32[2,2,36,192]{3,2,1,0:T(8,128)}, f32[2,2,36,192]{3,2,1,0:T(8,128)S(1)}, u32[]{:S(2)}) copy-start(f32[2,2,36,192]{3,2,1,0:T(8,128)S(1)} %select_add_fusion.2) | copy-start | bytes 331780 | tf_op jit(solution)/shard_map/while
  455.3 4.2 collective-permute-start
  456.6 4.7 collective-permute-start.1
  457.5 5.9 copy-start.2
  463.4 2.0 copy-start
  485.3 1.4 copy-start.4
  486.7 1.4 copy-start.5
  489.3 1.4 copy-start.3
  490.4 1.5 copy-start.6
  492.0 3.1 copy-start.11
  492.0 3.2 copy-start.1
  496.2 7.4 %copy-start.9 = (f32[2,2,36,192]{3,2,1,0:T(8,128)S(1)}, f32[2,2,36,192]{3,2,1,0:T(8,128)}, u32[]{:S(2)}) copy-start(f32[2,2,36,192]{3,2,1,0:T(8,128)} %get-tuple-element.359) | copy-start | bytes 331780 | tf_op jit(solution)/shard_map/while
  496.2 60.3 %copy-start.15 = (s32[1,2]{1,0:T(1,128)S(1)}, s32[1,2]{1,0:T(1,128)}, u32[]{:S(2)}) copy-start(s32[1,2]{1,0:T(1,128)} %get-tuple-element.407) | copy-start | bytes 28 | tf_op jit(solution)/shard_map/while
  501.7 54.8 %collective-permute-start.2 = (f32[2,36,36,192]{3,0,2,1:T(2,128)}, f32[2,36,36,192]{3,0,2,1:T(2,128)S(1)}, u32[]{:S(2)}, u32[]{:S(2)}) collective-permute-start(f32[2,36,36,192]{3,0,2,1:T(2,128)} %copy.48), channel_id=1, source_target_pairs={{4,0},{8,4},{12,8},{5,1},{9,5},{13,9},{6,2},{10,6},{14,10},{7,3},{... | collective-permute-start | bytes 5971976 | tf_op jit(solution)/shard_map/while/body/eval_jaxpr/ppermute | solution.py:24
  504.6 51.9 %copy-start.10 = (f32[2,2,36,192]{3,2,1,0:T(8,128)}, f32[2,2,36,192]{3,2,1,0:T(8,128)S(1)}, u32[]{:S(2)}) copy-start(f32[2,2,36,192]{3,2,1,0:T(8,128)S(1)} %select_add_fusion.2) | copy-start | bytes 331780 | tf_op jit(solution)/shard_map/while
  560.0 4.2 collective-permute-start
  561.3 4.7 collective-permute-start.1
  562.2 5.9 copy-start.2
  568.8 39.8 %copy-start.9 = (f32[2,2,36,192]{3,2,1,0:T(8,128)S(1)}, f32[2,2,36,192]{3,2,1,0:T(8,128)}, u32[]{:S(2)}) copy-start(f32[2,2,36,192]{3,2,1,0:T(8,128)} %get-tuple-element.359) | copy-start | bytes 331780 | tf_op jit(solution)/shard_map/while
  568.8 88.8 %copy-start.15 = (s32[1,2]{1,0:T(1,128)S(1)}, s32[1,2]{1,0:T(1,128)}, u32[]{:S(2)}) copy-start(s32[1,2]{1,0:T(1,128)} %get-tuple-element.407) | copy-start | bytes 28 | tf_op jit(solution)/shard_map/while
  574.2 83.4 %collective-permute-start.2 = (f32[2,36,36,192]{3,0,2,1:T(2,128)}, f32[2,36,36,192]{3,0,2,1:T(2,128)S(1)}, u32[]{:S(2)}, u32[]{:S(2)}) collective-permute-start(f32[2,36,36,192]{3,0,2,1:T(2,128)} %copy.48), channel_id=1, source_target_pairs={{4,0},{8,4},{12,8},{5,1},{9,5},{13,9},{6,2},{10,6},{14,10},{7,3},{... | collective-permute-start | bytes 5971976 | tf_op jit(solution)/shard_map/while/body/eval_jaxpr/ppermute | solution.py:24
  609.5 48.1 %copy-start.10 = (f32[2,2,36,192]{3,2,1,0:T(8,128)}, f32[2,2,36,192]{3,2,1,0:T(8,128)S(1)}, u32[]{:S(2)}) copy-start(f32[2,2,36,192]{3,2,1,0:T(8,128)S(1)} %select_add_fusion.2) | copy-start | bytes 331780 | tf_op jit(solution)/shard_map/while
Sparse Core Ops, SparseCore 0:
  659.9 23.1 reduce-scatter.3
where the time goes:
time: 700 us; the launch traced here: 692 us
  waiting for transfers between devices  312 us (45%)
  other arithmetic  245 us (35%)
  local copies, waits for them, and re-layouts  64.6 us (9%)
  starting transfers between devices  50 us (7%)
  between operations  13.6 us (2%)
    ppermute x4, waiting for transfers between devices, passed_along(): return lax.ppermute(block, axis, route)  272 us
    scatter-add x1, other arithmetic, on_device(): forcing = jnp.zeros((probes, limit), jnp.float32).at[:, places].add(bundl...  207 us
    ppermute x4, starting transfers between devices, passed_along(): return lax.ppermute(block, axis, route)  40.8 us
    unnamed x2, waiting for transfers between devices  23.3 us
    cond x4, local copies, waits for them, and re-layouts, sweep(): outgoing, flux_part = lax.cond(active, working, waiting, None)  21.9 us
  transfers between devices with their start and end apart: 17, of which 13 were waited for; matrix products, arithmetic and copies ran while one was open for 33% of the time, Pallas kernels for 0%

commit v1 on v0

v1 whole, which is shorter than its diff:
```python
import functools

import jax
import jax.numpy as jnp
from jax import lax
from jax.experimental import pallas as pl
from jax.experimental.pallas import tpu as pltpu
from jax.sharding import PartitionSpec as P


def split2(x):
    high = x.astype(jnp.bfloat16)
    low = (x - high.astype(jnp.float32)).astype(jnp.bfloat16)
    return high, low


def sweep_kernel(dims, weeks_ref, mix_ref, low_ref, own_ref, high_ref, obs_ref, out_ref, state, mixed, flux, wind):
    hours, hours_sec, halo, band_cols, lev, lev_pad, lat_rows, own, left, window, probes = dims
    ext_cols = band_cols + 2 * halo
    lanes = window * probes
    step = pl.program_id(0)
    hour = hours - 1 - step
    first_row = lax.axis_index("tm") * own - left

    @pl.when(step == 0)
    def _():
        state[...] = jnp.zeros_like(state)
        mixed[...] = jnp.zeros_like(mixed)
        flux[...] = jnp.zeros_like(flux)

    @pl.when(lax.rem(hour, hours_sec) == 0)
    def _():
        cols_at = 4
        count = obs_ref.shape[-1]
        for piece, (begin, width, shift) in enumerate(
            ((halo, band_cols, 0), (0, halo, -band_cols), (halo + band_cols, halo, band_cols))
        ):
            cell = obs_ref[0, piece, 0:1, :].astype(jnp.int32)
            level = cell // (band_cols * lat_rows)
            rest = cell - level * (band_cols * lat_rows)
            column = rest // lat_rows
            row = rest - column * lat_rows - first_row
            place = (column + halo + shift - begin) * lev_pad + level
            sub = lax.broadcasted_iota(jnp.int32, (window, count), 0)
            hit = sub == row
            parts = [
                split2(jnp.where(hit, obs_ref[0, piece, 1 + p : 2 + p, :], 0.0))
                for p in range(probes)
            ]
            rhs = jnp.concatenate([x[0] for x in parts] + [x[1] for x in parts], axis=0)
            chunk = lax.broadcasted_iota(jnp.int32, (cols_at * lev_pad, count), 0)

            def body(i, carry):
                hot = (chunk == place - i * (cols_at * lev_pad)).astype(jnp.float32)
                got = lax.dot_general(
                    hot.astype(jnp.bfloat16), rhs, (((1,), (1,)), ((), ())),
                    preferred_element_type=jnp.float32,
                )
                add = got[:, :lanes] + got[:, lanes:]
                for c in range(cols_at):
                    at = begin + i * cols_at + c
                    state[at] += add[c * lev_pad : (c + 1) * lev_pad]
                return carry

            lax.fori_loop(0, width // cols_at, body, 0)

    week = weeks_ref[hour]
    flux[week] += state[halo : halo + band_cols, 0, :]

    wind[:halo] = low_ref[0]
    wind[halo : halo + band_cols] = own_ref[0]
    wind[halo + band_cols :] = high_ref[0]
    mix = mix_ref[...]

    def mixing(i, carry):
        x = jnp.concatenate([state[2 * i], state[2 * i + 1]], axis=1)
        low = x - x.astype(jnp.bfloat16).astype(jnp.float32)
        stack = jnp.concatenate([x, x, low], axis=0).astype(jnp.bfloat16)
        got = jnp.dot(mix, stack, preferred_element_type=jnp.float32)
        mixed[2 * i] = got[:, :lanes]
        mixed[2 * i + 1] = got[:, lanes:]
        return carry

    lax.fori_loop(0, ext_cols // 2, mixing, 0, unroll=4)

    lane = lax.broadcasted_iota(jnp.int32, (lev_pad, lanes), 1)
    first = lane < window
    grid_row = lax.rem(lane, window) + first_row
    keep = jnp.logical_and(grid_row >= 0, grid_row < lat_rows - 1)

    def advect(j, carry):
        packed = wind[j].astype(jnp.float32)
        turned = pltpu.roll(packed, window, 1)
        before = wind[j - 1].astype(jnp.float32)
        east = jnp.where(first, packed, turned)
        west = jnp.where(first, before, pltpu.roll(before, window, 1))
        north = jnp.where(first, turned, packed)
        north = jnp.where(keep, north, 0.0)
        south = pltpu.roll(north, 1, 1)
        here = mixed[j]
        g = (
            here
            + jnp.maximum(east, 0.0) * (mixed[j + 1] - here)
            + jnp.minimum(west, 0.0) * (here - mixed[j - 1])
        )
        above = pltpu.roll(g, lanes - 1, 1)
        below = pltpu.roll(g, 1, 1)
        state[j] = g + jnp.maximum(north, 0.0) * (above - g) + jnp.minimum(south, 0.0) * (g - below)
        return carry

    lax.fori_loop(1, ext_cols - 1, advect, 0, unroll=2)

    @pl.when(step == hours - 1)
    def _():
        square = flux[...] * flux[...]
        rolled = [
            square[w] + pltpu.roll(square[w], lanes - window, 1) for w in range(square.shape[0])
        ]
        for w in range(square.shape[0]):
            out_ref[w] = rolled[w] * 0.5


def on_device(winds, mixing, obs_cell, obs_weight, probe_sign, week_map, prior_precision):
    hours_sec = winds.shape[2]
    levels = winds.shape[3]
    band_cols = winds.shape[4]
    lat_rows = winds.shape[5]
    probes = probe_sign.shape[0]
    week_count, _, own = prior_precision.shape
    sections = lax.axis_size("tm")
    bands = lax.axis_size("lon")
    hours = sections * hours_sec
    lev_pad = -(-levels // 8) * 8
    halo = -(-hours // 4) * 4
    left = hours
    window = -(-(own + 2 * hours) // 64) * 64
    lanes = window * probes

    w = winds[:, 0].transpose(1, 3, 2, 0, 4)
    w = jnp.pad(w, ((0, 0), (0, 0), (0, lev_pad - levels), (0, 0), (left, window - own - left)))
    w = jnp.stack([w[..., d * own : d * own + window] for d in range(sections)])
    w = w.reshape(sections, hours_sec, band_cols, lev_pad, 2 * window)
    w = lax.all_to_all(w, "tm", 0, 0, tiled=True)
    w = w.reshape(hours, band_cols, lev_pad, 2 * window)
    right_way = [(i, (i + 1) % bands) for i in range(bands)]
    left_way = [(b, a) for a, b in right_way]
    low = lax.ppermute(w[:, band_cols - halo :], "lon", right_way)
    high = lax.ppermute(w[:, :halo], "lon", left_way)

    value = (2 * probe_sign[:, 0, 0] - 1).astype(jnp.float32) * obs_weight[0, 0][None]
    bundle = jnp.concatenate([obs_cell[0, 0].astype(jnp.float32)[None], value], axis=0)
    bundle = lax.all_gather(bundle, "tm")
    from_low = lax.ppermute(bundle, "lon", right_way)
    from_high = from_low if bands == 2 else lax.ppermute(bundle, "lon", left_way)
    obs = jnp.stack([bundle, from_low, from_high], axis=1)
    weeks = lax.all_gather(week_map[0], "tm").reshape(hours)

    mix = jnp.pad(mixing.T, ((0, lev_pad - levels),) * 2)
    high_mix = lax.reduce_precision(mix, 8, 7)
    mix = jnp.concatenate([high_mix, mix - high_mix, high_mix], axis=1).astype(jnp.bfloat16)

    dims = (
        hours, hours_sec, halo, band_cols, levels, lev_pad, lat_rows, own, left, window, probes
    )
    ext_cols = band_cols + 2 * halo
    estimate = pl.pallas_call(
        functools.partial(sweep_kernel, dims),
        out_shape=jax.ShapeDtypeStruct((week_count, band_cols, lanes), jnp.float32),
        grid_spec=pltpu.PrefetchScalarGridSpec(
            num_scalar_prefetch=1,
            grid=(hours,),
            in_specs=[
                pl.BlockSpec(mix.shape, lambda i, wk: (0, 0)),
                *(
                    pl.BlockSpec((1,) + x.shape[1:], lambda i, wk: (hours - 1 - i, 0, 0, 0))
                    for x in (low, w, high)
                ),
                pl.BlockSpec(
                    (1,) + obs.shape[1:], lambda i, wk: ((hours - 1 - i) // hours_sec, 0, 0, 0)
                ),
            ],
            out_specs=pl.BlockSpec((week_count, band_cols, lanes), lambda i, wk: (0, 0, 0)),
            scratch_shapes=[
                pltpu.VMEM((ext_cols, lev_pad, lanes), jnp.float32),
                pltpu.VMEM((ext_cols, lev_pad, lanes), jnp.float32),
                pltpu.VMEM((week_count, band_cols, lanes), jnp.float32),
                pltpu.VMEM((ext_cols, lev_pad, 2 * window), jnp.bfloat16),
            ],
        ),
        compiler_params=pltpu.CompilerParams(vmem_limit_bytes=48 << 20),
    )(weeks, mix, low, w, high, obs)
    return (prior_precision + estimate[..., left : left + own])[None]


def solution(mesh):
    placed = (
        P(None, ("groups", "tm"), None, None, "lon", None),
        P(),
        P(("groups", "tm"), "lon", None),
        P(("groups", "tm"), "lon", None),
        P("probe", ("groups", "tm"), "lon", None),
        P(("groups", "tm"), None),
        P("groups", "lon", "tm"),
    )
    return jax.shard_map(
        on_device,
        mesh=mesh,
        in_specs=placed,
        out_specs=P("probe", "groups", "lon", "tm"),
        check_vma=False,
    )
```

time: 700 us -> 224 us (0.32)
  the two profiles are of different devices: /device:TPU:9 before, /device:TPU:0 now
where the time goes in v1:
time: 224 us; the launch traced here: 223 us
  Pallas kernels  77.4 us (35%)
  waiting for transfers between devices  71.7 us (32%)
  local copies, waits for them, and re-layouts  37.4 us (17%)
  blocking collectives  22.4 us (10%)
  starting transfers between devices  9.98 us (4%)
  other arithmetic  3.95 us (2%)
    pallas_call x1, Pallas kernels, on_device(): pl.pallas_call(functools.partial(sweep_kernel, dims), out_shape=jax.Shape...  77.4 us
    all_to_all x1, waiting for transfers between devices, on_device(): w = lax.all_to_all(w, 'tm', 0, 0, tiled=True)  66.4 us
    slice x5, local copies, waits for them, and re-layouts, on_device(): w = jnp.stack([w[..., d * own:d * own + window] for d in range(sections)])  22.8 us
    all_gather x1, blocking collectives, on_device(): bundle = lax.all_gather(bundle, 'tm')  13.3 us
    another operation x4, local copies, waits for them, and re-layouts, on_device(): w = jnp.stack([w[..., d * own:d * own + window] for d in range(sections)])  11.9 us
    all_gather x1, blocking collectives, on_device(): weeks = lax.all_gather(week_map[0], 'tm').reshape(hours)  9.08 us
    all_to_all x1, starting transfers between devices, on_device(): w = lax.all_to_all(w, 'tm', 0, 0, tiled=True)  6.46 us
    ppermute x1, waiting for transfers between devices, on_device(): from_low = lax.ppermute(bundle, 'lon', right_way)  5.34 us
  transfers between devices with their start and end apart: 4, of which 2 were waited for; matrix products, arithmetic and copies ran while one was open for 1% of the time, Pallas kernels for 0%

profile of v1, /device:TPU:0, one launch (start us, length us, event | category | flops | bytes accessed | tf_op | source)
XLA Modules:
  0.0 223.0 jit_solution(16763989641425779534)
XLA Ops:
  0.0 12.0 %pad_slice_fusion.3 = (bf16[2,36,40,2,64]{4,0,1,2,3:T(2,128)(2,1)S(1)}, bf16[2,36,40,2,64]{4,0,1,2,3:T(2,128)(2,1)}, bf16[2,36,40,2,64]{4,0,1,2,3:T(2,128)(2,1)S(1)}, bf16[2,36,40,2,64]{4,0,1,2,3:T(2,128)(2,1)S(1)}) fusion(bf16[2,36,36,2,192]{4,0,1,2,3:T(2,128)(2,1)} %bitcast.19), kind=kLoop, calls=%fused_computation.17 | loop fusion | bytes 4939776 | tf_op jit(solution)/shard_map/slice | solution.py:141
  12.0 2.6 %copy.23 = bf16[2,36,40,2,64]{4,3,2,1,0:T(2,128)(2,1)} copy(bf16[2,36,40,2,64]{4,0,1,2,3:T(2,128)(2,1)S(1)} %get-tuple-element.7) | data formatting | bytes 1474560 | tf_op jit(solution)/shard_map/slice | solution.py:141
  14.7 3.7 %stack.25 = bf16[1,2,36,40,128]{4,3,2,1,0:T(8,128)(2,1)} reshape(bf16[2,36,40,2,64]{4,3,2,1,0:T(2,128)(2,1)} %copy.23) | data formatting | bytes 1474560 | tf_op jit(solution)/shard_map/stack | solution.py:141
  18.4 4.0 %copy.24 = bf16[2,36,40,2,64]{4,3,2,1,0:T(2,128)(2,1)} copy(bf16[2,36,40,2,64]{4,0,1,2,3:T(2,128)(2,1)} %get-tuple-element.8) | data formatting | bytes 1474560 | tf_op jit(solution)/shard_map/slice | solution.py:141
  22.4 3.7 %stack.26 = bf16[1,2,36,40,128]{4,3,2,1,0:T(8,128)(2,1)} reshape(bf16[2,36,40,2,64]{4,3,2,1,0:T(2,128)(2,1)} %copy.24) | data formatting | bytes 1474560 | tf_op jit(solution)/shard_map/stack | solution.py:141
  26.1 2.6 %copy.25 = bf16[2,36,40,2,64]{4,3,2,1,0:T(2,128)(2,1)} copy(bf16[2,36,40,2,64]{4,0,1,2,3:T(2,128)(2,1)S(1)} %get-tuple-element.9) | data formatting | bytes 1474560 | tf_op jit(solution)/shard_map/slice | solution.py:141
  28.7 3.7 %stack.27 = bf16[1,2,36,40,128]{4,3,2,1,0:T(8,128)(2,1)} reshape(bf16[2,36,40,2,64]{4,3,2,1,0:T(2,128)(2,1)} %copy.25) | data formatting | bytes 1474560 | tf_op jit(solution)/shard_map/stack | solution.py:141
  32.4 1.5 copy.26
  33.9 0.8 stack.28
  34.8 3.0 %pad_maximum_fusion = bf16[4,2,36,40,128]{4,3,2,1,0:T(8,128)(2,1)} fusion(bf16[1,2,36,40,128]{4,3,2,1,0:T(8,128)(2,1)S(1)} %stack.28, bf16[1,2,36,40,128]{4,3,2,1,0:T(8,128)(2,1)} %stack.27, bf16[1,2,36,40,128]{4,3,2,1,0:T(8,128)(2,1)} %stack.26, bf16[1,2,36,40,128]{4,3,2,1,0:T(8,128)(2,1)} %stack.25), kind=kLoop, calls=%fused_computation | loop fusion | flops 4423680 | bytes 5898240 | tf_op jit(solution)/shard_map/stack | solution.py:141
  37.8 0.0 copy-start.4
  37.8 0.0 copy-start.2
  37.8 0.0 copy-start.3
  37.8 0.0 copy-start.5
  37.8 0.0 copy-start.1
  37.8 6.5 %all-to-all-start = ((bf16[4,2,36,40,128]{4,3,2,1,0:T(8,128)(2,1)}), bf16[4,2,36,40,128]{4,3,2,1,0:T(8,128)(2,1)S(1)}, u32[]{:S(2)}, u32[]{:S(2)}) async-start(bf16[4,2,36,40,128]{4,3,2,1,0:T(8,128)(2,1)} %pad_maximum_fusion), calls=%async_computation | async-start | bytes 5898240 | tf_op jit(solution)/shard_map/all_to_all | solution.py:143
  44.3 0.0 copy-done.4
  44.3 0.0 copy-done.2
  44.3 0.0 copy-done.3
  44.3 66.4 %all-to-all-done = bf16[4,2,36,40,128]{4,3,2,1,0:T(8,128)(2,1)S(1)} async-done(((bf16[4,2,36,40,128]{4,3,2,1,0:T(8,128)(2,1)}), bf16[4,2,36,40,128]{4,3,2,1,0:T(8,128)(2,1)S(1)}, u32[]{:S(2)}, u32[]{:S(2)}) %all-to-all-start) | async-done | bytes 2949152 | tf_op jit(solution)/shard_map/all_to_all | solution.py:143
  110.7 1.3 fusion.4
  112.0 0.0 copy-start
  112.0 1.5 collective-permute-start
  113.5 0.5 collective-permute-start.1
  114.0 13.3 %all-gather.2 = f32[4,3,2048]{2,1,0:T(4,128)S(1)} all-gather(f32[1,3,2048]{2,1,0:T(4,128)S(1)} %maximum_bitcast_fusion), channel_id=2, replica_groups=mesh['groups'=2,'tm'=4,'lon'=2,'probe'=2] {'tm'}, dimensions={0}, use_global_device_ids=true | all-gather | bytes 122880 | tf_op jit(solution)/shard_map/all_gather | solution.py:152
  127.4 1.5 collective-permute-start.2
  128.9 0.0 copy-done.5
  128.9 9.1 %all-gather.1 = s32[4,1,2]{2,1,0:T(1,128)S(1)} all-gather(s32[1,1,2]{2,1,0:T(1,128)S(1)} %bitcast.24), channel_id=1, replica_groups=mesh['groups'=2,'tm'=4,'lon'=2,'probe'=2] {'tm'}, dimensions={0}, use_global_device_ids=true | all-gather | bytes 40 | tf_op jit(solution)/shard_map/all_gather | solution.py:156
  137.9 0.0 copy-done.1
  137.9 0.1 copy.22
  138.0 0.5 broadcast.16
  138.6 0.7 reduce.3
  139.2 0.1 reshape.32.weeks_ref
  139.3 0.1 pad_maximum_fusion.2.mix_ref
  139.4 5.3 %collective-permute-done.2 = f32[4,3,2048]{2,1,0:T(4,128)S(1)} collective-permute-done((f32[4,3,2048]{2,1,0:T(4,128)S(1)}, f32[4,3,2048]{2,1,0:T(4,128)S(1)}, u32[]{:S(2)}, u32[]{:S(2)}) %collective-permute-start.2) | collective-permute-done | bytes 98336 | tf_op jit(solution)/shard_map/ppermute | solution.py:153
  144.7 0.1 pad_maximum_fusion.1.obs_ref
  144.8 0.0 collective-permute-done.low_ref
  144.8 0.0 collective-permute-done.1.high_ref
  144.9 77.4 %shard_map.73 = f32[2,36,128]{2,1,0:T(8,128)S(1)} custom-call(s32[8]{0:T(128)S(1)} %reshape.32.weeks_ref, bf16[40,120]{1,0:T(8,128)(2,1)S(1)} %pad_maximum_fusion.2.mix_ref, bf16[8,8,40,128]{3,2,1,0:T(8,128)(2,1)} %collective-permute-done.low_ref, bf16[8,36,40,128]{3,2,1,0:T(8,128)(2,1)S(1)} %bitcast.18, ...), custom_call_target="tpu_custom_call" | custom-call | tf_op jit(solution)/shard_map/pallas_call | solution.py:166
  222.3 0.0 copy-done
  222.3 0.1 fusion
  222.4 0.6 copy.29
  (4 shorter events, 0.1 us)
Async XLA Ops:
  37.8 6.5 %copy-start.4 = (s32[1,1,2048]{2,1,0:T(1,128)S(1)}, s32[1,1,2048]{2,1,0:T(1,128)}, u32[]{:S(2)}) copy-start(s32[1,1,2048]{2,1,0:T(1,128)} %param.9) | copy-start | bytes 24580
  37.8 6.5 %copy-start.2 = (s32[2,1,1,2048]{3,2,1,0:T(1,128)S(1)}, s32[2,1,1,2048]{3,2,1,0:T(1,128)}, u32[]{:S(2)}) copy-start(s32[2,1,1,2048]{3,2,1,0:T(1,128)} %param.11) | copy-start | bytes 49156
  37.8 6.5 %copy-start.3 = (f32[1,1,2048]{2,1,0:T(1,128)S(1)}, f32[1,1,2048]{2,1,0:T(1,128)}, u32[]{:S(2)}) copy-start(f32[1,1,2048]{2,1,0:T(1,128)} %param.10) | copy-start | bytes 24580
  37.8 91.1 %copy-start.5 = (s32[1,2]{1,0:T(1,128)S(1)}, s32[1,2]{1,0:T(1,128)}, u32[]{:S(2)}) copy-start(s32[1,2]{1,0:T(1,128)} %param.12) | copy-start | bytes 28
  37.8 100.2 %copy-start.1 = (f32[36,36]{1,0:T(8,128)S(1)}, f32[36,36]{1,0:T(8,128)}, u32[]{:S(2)}) copy-start(f32[36,36]{1,0:T(8,128)} %param.8) | copy-start | bytes 15556
  37.8 72.9 %all-to-all-start = ((bf16[4,2,36,40,128]{4,3,2,1,0:T(8,128)(2,1)}), bf16[4,2,36,40,128]{4,3,2,1,0:T(8,128)(2,1)S(1)}, u32[]{:S(2)}, u32[]{:S(2)}) async-start(bf16[4,2,36,40,128]{4,3,2,1,0:T(8,128)(2,1)} %pad_maximum_fusion), calls=%async_computation | async-start | bytes 5898240 | tf_op jit(solution)/shard_map/all_to_all | solution.py:143
  112.0 110.3 %copy-start = (f32[2,36,48]{2,0,1:T(2,128)S(1)}, f32[2,36,48]{2,0,1:T(2,128)}, u32[]{:S(2)}) copy-start(f32[2,36,48]{2,0,1:T(2,128)} %param.13) | copy-start | bytes 41476
  112.0 32.9 %collective-permute-start = (bf16[8,8,40,128]{3,2,1,0:T(8,128)(2,1)}, bf16[8,8,40,128]{3,2,1,0:T(8,128)(2,1)}, u32[]{:S(2)}, u32[]{:S(2)}) collective-permute-start(bf16[8,8,40,128]{3,2,1,0:T(8,128)(2,1)} %get-tuple-element.6), channel_id=1, source_target_pairs={{0,2},{2,0},{1,3},{3,1},{4,6},{6,4},{5,7},{7,5},{8,10},{10,8},{9,1... | collective-permute-start | bytes 1966088 | tf_op jit(solution)/shard_map/ppermute | solution.py:147
  113.5 31.4 %collective-permute-start.1 = (bf16[8,8,40,128]{3,2,1,0:T(8,128)(2,1)}, bf16[8,8,40,128]{3,2,1,0:T(8,128)(2,1)}, u32[]{:S(2)}, u32[]{:S(2)}) collective-permute-start(bf16[8,8,40,128]{3,2,1,0:T(8,128)(2,1)} %get-tuple-element.5), channel_id=1, source_target_pairs={{2,0},{0,2},{3,1},{1,3},{6,4},{4,6},{7,5},{5,7},{10,8},{8,10},{11,... | collective-permute-start | bytes 1966088 | tf_op jit(solution)/shard_map/ppermute | solution.py:148
  127.4 17.4 %collective-permute-start.2 = (f32[4,3,2048]{2,1,0:T(4,128)S(1)}, f32[4,3,2048]{2,1,0:T(4,128)S(1)}, u32[]{:S(2)}, u32[]{:S(2)}) collective-permute-start(f32[4,3,2048]{2,1,0:T(4,128)S(1)} %all-gather.2), channel_id=1, source_target_pairs={{0,2},{2,0},{1,3},{3,1},{4,6},{6,4},{5,7},{7,5},{8,10},{10,8},{9,1... | collective-permute-start | bytes 294920 | tf_op jit(solution)/shard_map/ppermute | solution.py:153

commit v2 on v1

v2 whole, which is shorter than its diff:
```python
import functools

import jax
import jax.numpy as jnp
from jax import lax
from jax.experimental import pallas as pl
from jax.experimental.pallas import tpu as pltpu
from jax.sharding import PartitionSpec as P


def split2(x):
    high = x.astype(jnp.bfloat16)
    low = (x - high.astype(jnp.float32)).astype(jnp.bfloat16)
    return high, low


def sweep_kernel(dims, weeks_ref, mix_ref, winds_ref, obs_ref, out_ref, state, mixed, flux):
    hours, hours_sec, halo, band_cols, lev, lev_pad, lat_rows, own, left, window, probes = dims
    ext_cols = band_cols + 2 * halo
    lanes = window * probes
    step = pl.program_id(0)
    hour = hours - 1 - step
    first_row = lax.axis_index("tm") * own - left

    @pl.when(step == 0)
    def _():
        state[...] = jnp.zeros_like(state)
        mixed[...] = jnp.zeros_like(mixed)
        flux[...] = jnp.zeros_like(flux)

    @pl.when(lax.rem(hour, hours_sec) == 0)
    def _():
        cols_at = 4
        count = obs_ref.shape[-1]
        for piece, (begin, width, shift) in enumerate(
            ((halo, band_cols, 0), (0, halo, -band_cols), (halo + band_cols, halo, band_cols))
        ):
            cell = obs_ref[0, piece, 0:1, :].astype(jnp.int32)
            level = cell // (band_cols * lat_rows)
            rest = cell - level * (band_cols * lat_rows)
            column = rest // lat_rows
            row = rest - column * lat_rows - first_row
            place = (column + halo + shift - begin) * lev_pad + level
            sub = lax.broadcasted_iota(jnp.int32, (window, count), 0)
            hit = sub == row
            parts = [
                split2(jnp.where(hit, obs_ref[0, piece, 1 + p : 2 + p, :], 0.0))
                for p in range(probes)
            ]
            rhs = jnp.concatenate([x[0] for x in parts] + [x[1] for x in parts], axis=0)
            chunk = lax.broadcasted_iota(jnp.int32, (cols_at * lev_pad, count), 0)

            def body(i, carry):
                hot = (chunk == place - i * (cols_at * lev_pad)).astype(jnp.float32)
                got = lax.dot_general(
                    hot.astype(jnp.bfloat16), rhs, (((1,), (1,)), ((), ())),
                    preferred_element_type=jnp.float32,
                )
                add = got[:, :lanes] + got[:, lanes:]
                for c in range(cols_at):
                    at = begin + i * cols_at + c
                    state[at] += add[c * lev_pad : (c + 1) * lev_pad]
                return carry

            lax.fori_loop(0, width // cols_at, body, 0)

    week = weeks_ref[hour]
    flux[week] += state[halo : halo + band_cols, 0, :]

    @pl.when(hour > 0)
    def _():
        mix = mix_ref[...]

        def mixing(i, carry):
            x = jnp.concatenate([state[2 * i], state[2 * i + 1]], axis=1)
            low = x - x.astype(jnp.bfloat16).astype(jnp.float32)
            stack = jnp.concatenate([x, x, low], axis=0).astype(jnp.bfloat16)
            got = jnp.dot(mix, stack, preferred_element_type=jnp.float32)
            mixed[2 * i] = got[:, :lanes]
            mixed[2 * i + 1] = got[:, lanes:]
            return carry

        lax.fori_loop(0, ext_cols // 2, mixing, 0, unroll=4)

        lane = lax.broadcasted_iota(jnp.int32, (lev_pad, lanes), 1)
        first = lane < window
        grid_row = lax.rem(lane, window) + first_row
        keep = jnp.logical_and(grid_row >= 0, grid_row < lat_rows - 1)

        def advect(j, carry):
            packed = winds_ref[0, j].astype(jnp.float32)
            turned = pltpu.roll(packed, window, 1)
            before = winds_ref[0, j - 1].astype(jnp.float32)
            east = jnp.where(first, packed, turned)
            west = jnp.where(first, before, pltpu.roll(before, window, 1))
            north = jnp.where(first, turned, packed)
            north = jnp.where(keep, north, 0.0)
            south = pltpu.roll(north, 1, 1)
            here = mixed[j]
            g = (
                here
                + jnp.maximum(east, 0.0) * (mixed[j + 1] - here)
                + jnp.minimum(west, 0.0) * (here - mixed[j - 1])
            )
            above = pltpu.roll(g, lanes - 1, 1)
            below = pltpu.roll(g, 1, 1)
            state[j] = g + jnp.maximum(north, 0.0) * (above - g) + jnp.minimum(south, 0.0) * (g - below)
            return carry

        lax.fori_loop(1, ext_cols - 1, advect, 0, unroll=2)

    @pl.when(step == hours - 1)
    def _():
        square = flux[...] * flux[...]
        rolled = [
            square[w] + pltpu.roll(square[w], lanes - window, 1) for w in range(square.shape[0])
        ]
        for w in range(square.shape[0]):
            out_ref[w] = rolled[w] * 0.5


def window_kernel(dims, winds_ref, out_ref, *tmp):
    lev, lev_pad, cols, lat, own, left, window = dims
    d = pl.program_id(1)
    wide = -(-lat // 128) * 128
    shift = lax.rem(left - d * own + 2 * wide, wide)
    row = lax.broadcasted_iota(jnp.int32, (cols, wide), 1)
    fill = jnp.zeros((cols, wide - lat), jnp.float32)

    for part in tmp:
        part[...] = jnp.zeros_like(part)

    def level(i, carry):
        moved = []
        for comp in range(2):
            x = jnp.concatenate([winds_ref[comp, 0, 0, i].astype(jnp.float32), fill], axis=1)
            at = row - comp * window
            at_row = at + d * own - left
            inside = (at >= 0) & (at < window) & (at_row >= 0) & (at_row < lat)
            turn = shift + comp * window
            turn = jnp.where(turn >= wide, turn - wide, turn)
            moved.append(jnp.where(inside, pltpu.roll(x, turn, 1), 0.0))
        both = moved[0] + moved[1]
        for n, part in enumerate(tmp):
            part[pl.ds(i, cols, stride=lev_pad), :] = both[:, n * 128 : (n + 1) * 128]
        return carry

    lax.fori_loop(0, lev, level, 0, unroll=2)

    def column(c, carry):
        for n, part in enumerate(tmp):
            block = part[pl.ds(pl.multiple_of(c * lev_pad, 8), lev_pad), :]
            out_ref[0, 0, c, :, n * 128 : (n + 1) * 128] = block.astype(jnp.bfloat16)
        return carry

    lax.fori_loop(0, cols, column, 0, unroll=4)


def spread_kernel(dims, pack, bundle, winds, obs, zs, zr, xs, xr, hs, hr, gs, gr, os, orr, local):
    sections, bands, cols, halo = dims
    me = lax.axis_index("tm")
    band = lax.axis_index("lon")
    core = lax.axis_index("probe")
    half = cols // 2
    sides = (band, lax.rem(band + 1, bands), lax.rem(band + bands - 1, bands))

    def remote(src, dst, send, recv, tm, lon, probe):
        copy = pltpu.make_async_remote_copy(
            src_ref=src, dst_ref=dst, send_sem=send, recv_sem=recv,
            device_id={"tm": tm, "lon": lon, "probe": probe},
            device_id_type=pl.DeviceIdType.MESH,
        )
        copy.start()
        return copy

    barrier = pltpu.get_barrier_semaphore()
    for k in range(sections):
        tm = lax.rem(me + k, sections)
        for n, lon in enumerate(sides):
            if k or n:
                pl.semaphore_signal(
                    barrier, inc=1, device_id={"tm": tm, "lon": lon, "probe": core},
                    device_id_type=pl.DeviceIdType.MESH,
                )
    pl.semaphore_signal(
        barrier, inc=1, device_id={"tm": me, "lon": band, "probe": 1 - core},
        device_id_type=pl.DeviceIdType.MESH,
    )
    own_winds = pltpu.make_async_copy(pack.at[me], winds.at[me, :, pl.ds(halo, cols)], local.at[0])
    own_winds.start()
    own_obs = pltpu.make_async_copy(bundle, obs.at[me, 0], local.at[1])
    own_obs.start()
    pl.semaphore_wait(barrier, 3 * sections)

    mine = pl.ds(halo + half * core, half)
    edge = pl.ds((1 - core) * (halo + cols), halo)
    beside = lax.rem(band + bands + 2 * core - 1, bands)
    z_copies, x_copies, h_copies, g_copies, o_copies = [], [], [], [], []
    for k in range(1, sections):
        tm = lax.rem(me + k, sections)
        z_copies.append(
            remote(
                pack.at[tm, :, pl.ds(half * core, half)], winds.at[me, :, mine],
                zs.at[k], zr.at[k], tm, band, core,
            )
        )
    for k in range(sections):
        tm = lax.rem(me + k, sections)
        for n, lon in enumerate(sides):
            if k or n:
                o_copies.append(
                    remote(
                        bundle, obs.at[me, n], os.at[3 * k + n], orr.at[3 * k + n], tm, lon, core
                    )
                )
    x_copies.append(
        remote(
            pack.at[me, :, pl.ds(core * (cols - halo), halo)], winds.at[me, :, edge],
            xs.at[0], xr.at[0], me, beside, core,
        )
    )
    for k in range(1, sections):
        source = lax.rem(me + sections - k, sections)
        z_copies[k - 1].wait_recv()
        h_copies.append(
            remote(
                winds.at[source, :, mine], winds.at[source, :, mine],
                hs.at[k], hr.at[k], me, band, 1 - core,
            )
        )
        if halo > half:
            h_copies[-1].wait_recv()
        x_copies.append(
            remote(
                winds.at[source, :, pl.ds(halo + core * (cols - halo), halo)],
                winds.at[source, :, edge], xs.at[k], xr.at[k], me, beside, core,
            )
        )
    for k in range(sections):
        source = lax.rem(me + sections - k, sections)
        x_copies[k].wait_recv()
        g_copies.append(
            remote(
                winds.at[source, :, edge], winds.at[source, :, edge],
                gs.at[k], gr.at[k], me, band, 1 - core,
            )
        )
    if halo <= half:
        for copy in h_copies:
            copy.wait_recv()
    for copy in g_copies + o_copies:
        copy.wait_recv()
    for copy in z_copies + x_copies + h_copies + g_copies + o_copies:
        copy.wait_send()
    own_winds.wait()
    own_obs.wait()


def on_device(winds, mixing, obs_cell, obs_weight, probe_sign, week_map, prior_precision):
    hours_sec = winds.shape[2]
    levels = winds.shape[3]
    band_cols = winds.shape[4]
    lat_rows = winds.shape[5]
    probes = probe_sign.shape[0]
    week_count, _, own = prior_precision.shape
    sections = lax.axis_size("tm")
    bands = lax.axis_size("lon")
    hours = sections * hours_sec
    lev_pad = -(-levels // 8) * 8
    halo = -(-hours // 4) * 4
    left = hours
    window = -(-(own + 2 * hours) // 64) * 64
    lanes = window * probes

    shape = (hours_sec, sections, band_cols, lev_pad, 2 * window)
    pack = pl.pallas_call(
        functools.partial(
            window_kernel, (levels, lev_pad, band_cols, lat_rows, own, left, window)
        ),
        out_shape=jax.ShapeDtypeStruct((sections, hours_sec) + shape[2:], jnp.bfloat16),
        grid=(hours_sec, sections),
        in_specs=[
            pl.BlockSpec(
                (2, 1, 1, levels, band_cols, lat_rows), lambda h, d: (0, 0, h, 0, 0, 0)
            )
        ],
        out_specs=pl.BlockSpec((1, 1) + shape[2:], lambda h, d: (d, h, 0, 0, 0)),
        scratch_shapes=[pltpu.VMEM((band_cols * lev_pad, 128), jnp.float32)]
        * (2 * window // 128),
        compiler_params=pltpu.CompilerParams(vmem_limit_bytes=40 << 20),
    )(winds)

    value = (2 * probe_sign[:, 0, 0] - 1).astype(jnp.float32) * obs_weight[0, 0][None]
    count = value.shape[1]
    week_row = jnp.pad(week_map.astype(jnp.float32), ((0, 0), (0, count - hours_sec)))
    bundle = jnp.concatenate([obs_cell[0].astype(jnp.float32), value, week_row], axis=0)
    ext_cols = band_cols + 2 * halo
    sem = pltpu.SemaphoreType.DMA
    w, obs = pl.pallas_call(
        functools.partial(spread_kernel, (sections, bands, band_cols, halo)),
        out_shape=(
            jax.ShapeDtypeStruct(
                (sections, hours_sec, ext_cols, lev_pad, 2 * window), jnp.bfloat16
            ),
            jax.ShapeDtypeStruct((sections, 3) + bundle.shape, jnp.float32),
        ),
        in_specs=[pl.BlockSpec(memory_space=pl.ANY)] * 2,
        out_specs=(pl.BlockSpec(memory_space=pl.ANY),) * 2,
        scratch_shapes=[sem((sections,))] * 8 + [sem((3 * sections,))] * 2 + [sem((2,))],
        compiler_params=pltpu.CompilerParams(collective_id=0, has_side_effects=True),
    )(pack, bundle)
    w = w.reshape((hours,) + w.shape[2:])
    weeks = obs[:, 0, 1 + probes, :hours_sec].astype(jnp.int32).reshape(hours)

    mix = jnp.pad(mixing.T, ((0, lev_pad - levels),) * 2)
    high_mix = lax.reduce_precision(mix, 8, 7)
    mix = jnp.concatenate([high_mix, mix - high_mix, high_mix], axis=1).astype(jnp.bfloat16)

    dims = (
        hours, hours_sec, halo, band_cols, levels, lev_pad, lat_rows, own, left, window, probes
    )
    estimate = pl.pallas_call(
        functools.partial(sweep_kernel, dims),
        out_shape=jax.ShapeDtypeStruct((week_count, band_cols, lanes), jnp.float32),
        grid_spec=pltpu.PrefetchScalarGridSpec(
            num_scalar_prefetch=1,
            grid=(hours,),
            in_specs=[
                pl.BlockSpec(mix.shape, lambda i, wk: (0, 0)),
                pl.BlockSpec((1,) + w.shape[1:], lambda i, wk: (hours - 1 - i, 0, 0, 0)),
                pl.BlockSpec(
                    (1,) + obs.shape[1:], lambda i, wk: ((hours - 1 - i) // hours_sec, 0, 0, 0)
                ),
            ],
            out_specs=pl.BlockSpec((week_count, band_cols, lanes), lambda i, wk: (0, 0, 0)),
            scratch_shapes=[
                pltpu.VMEM((ext_cols, lev_pad, lanes), jnp.float32),
                pltpu.VMEM((ext_cols, lev_pad, lanes), jnp.float32),
                pltpu.VMEM((week_count, band_cols, lanes), jnp.float32),
            ],
        ),
        compiler_params=pltpu.CompilerParams(vmem_limit_bytes=48 << 20),
    )(weeks, mix, w, obs)
    return (prior_precision + estimate[..., left : left + own])[None]


def solution(mesh):
    placed = (
        P(None, ("groups", "tm"), None, None, "lon", None),
        P(),
        P(("groups", "tm"), "lon", None),
        P(("groups", "tm"), "lon", None),
        P("probe", ("groups", "tm"), "lon", None),
        P(("groups", "tm"), None),
        P("groups", "lon", "tm"),
    )
    return jax.shard_map(
        on_device,
        mesh=mesh,
        in_specs=placed,
        out_specs=P("probe", "groups", "lon", "tm"),
        check_vma=False,
    )
```

time: 224 us -> 148 us (0.66)
  the two profiles are of different devices: /device:TPU:0 before, /device:TPU:9 now
where the time goes in v2:
time: 148 us; the launch traced here: 145 us
  Pallas kernels  135 us (91%)
  local copies, waits for them, and re-layouts  7.81 us (5%)
  other arithmetic  1.56 us (1%)
    pallas_call x1, Pallas kernels, on_device(): pl.pallas_call(functools.partial(sweep_kernel, dims), out_shape=jax.Shape...  70.7 us
    pallas_call x1, Pallas kernels, on_device(): pl.pallas_call(functools.partial(spread_kernel, (sections, bands, band_co...  49.4 us
    pallas_call x1, Pallas kernels, on_device(): pl.pallas_call(functools.partial(window_kernel, (levels, lev_pad, band_co...  15.1 us
    unnamed x20, local copies, waits for them, and re-layouts  7.09 us

profile of v2, /device:TPU:9, one launch (start us, length us, event | category | flops | bytes accessed | tf_op | source)
XLA Modules:
  0.0 144.7 jit_solution(4247567353619741062)
XLA Ops:
  0.0 2.2 %copy.13.winds_ref = bf16[2,1,2,36,36,192]{5,4,3,2,1,0:T(8,128)(2,1)S(1)} copy(bf16[2,1,2,36,36,192]{5,2,4,3,1,0:T(2,128)(2,1)} %param.7) | data formatting | bytes 3981312 | tf_op args[0]
  2.2 0.0 copy-start.5
  2.2 0.0 copy-start.6
  2.2 0.0 copy-start.7
  2.2 0.0 copy-start.8
  2.2 15.1 %shard_map.73.pack = bf16[4,2,36,40,128]{4,3,2,1,0:T(8,128)(2,1)S(1)} custom-call(bf16[2,1,2,36,36,192]{5,4,3,2,1,0:T(8,128)(2,1)S(1)} %copy.13.winds_ref), custom_call_target="tpu_custom_call" | custom-call | tf_op jit(solution)/shard_map/pallas_call | solution.py:276
  17.3 0.0 copy-start
  17.3 1.6 %copy-done = bf16[4,2,36,40,128]{4,3,2,1,0:T(8,128)(2,1)} copy-done((bf16[4,2,36,40,128]{4,3,2,1,0:T(8,128)(2,1)}, bf16[4,2,36,40,128]{4,3,2,1,0:T(8,128)(2,1)S(1)}, u32[]{:S(2)}) %copy-start) | copy-done | bytes 2949144
  18.9 0.0 copy-start.4
  18.9 0.0 copy-done.5
  18.9 0.0 copy-done.6
  18.9 0.0 copy-done.7
  19.0 0.0 copy-done.8
  19.0 0.6 select_maximum_fusion.bundle
  19.6 49.4 %shard_map.74 = (bf16[4,2,52,40,128]{4,3,2,1,0:T(8,128)(2,1)}, f32[4,3,4,2048]{3,2,1,0:T(4,128)}) custom-call(bf16[4,2,36,40,128]{4,3,2,1,0:T(8,128)(2,1)} %copy-done, f32[4,2048]{1,0:T(4,128)} %select_maximum_fusion.bundle), custom_call_target="tpu_custom_call" | custom-call | tf_op jit(solution)/shard_map/pallas_call | solution.py:299
  69.1 0.0 copy-start.3
  69.1 0.7 convert_reduce_fusion
  69.8 0.1 convert_element_type.41.weeks_ref
  69.9 0.0 copy-done.4
  69.9 0.1 copy.15
  70.0 0.1 pad_maximum_fusion.mix_ref
  70.1 0.0 copy-start.1
  70.1 2.2 %copy-done.1 = bf16[4,2,52,40,128]{4,3,2,1,0:T(8,128)(2,1)S(1)} copy-done((bf16[4,2,52,40,128]{4,3,2,1,0:T(8,128)(2,1)S(1)}, bf16[4,2,52,40,128]{4,3,2,1,0:T(8,128)(2,1)}, u32[]{:S(2)}) %copy-start.1) | copy-done | bytes 4259864
  72.3 0.0 copy-start.2
  72.3 1.0 copy-done.2
  73.3 70.7 %shard_map.75 = f32[2,36,128]{2,1,0:T(8,128)S(1)} custom-call(s32[8]{0:T(128)S(1)} %convert_element_type.41.weeks_ref, bf16[40,120]{1,0:T(8,128)(2,1)S(1)} %pad_maximum_fusion.mix_ref, bf16[8,52,40,128]{3,2,1,0:T(8,128)(2,1)S(1)} %bitcast.9, f32[4,3,4,2048]{3,2,1,0:T(4,128)S(1)} %copy-done.2), custom_call_target="tpu_custom_call" | custom-call | tf_op jit(solution)/shard_map/pallas_call | solution.py:322
  144.0 0.0 copy-done.3
  144.0 0.1 fusion
  144.1 0.6 copy.17
  (4 shorter events, 0.0 us)
Async XLA Ops:
  2.2 16.8 %copy-start.5 = (s32[2,1,1,2048]{3,2,1,0:T(1,128)S(1)}, s32[2,1,1,2048]{3,2,1,0:T(1,128)}, u32[]{:S(2)}) copy-start(s32[2,1,1,2048]{3,2,1,0:T(1,128)} %param.11) | copy-start | bytes 49156
  2.2 16.8 %copy-start.6 = (f32[1,1,2048]{2,1,0:T(1,128)S(1)}, f32[1,1,2048]{2,1,0:T(1,128)}, u32[]{:S(2)}) copy-start(f32[1,1,2048]{2,1,0:T(1,128)} %param.10) | copy-start | bytes 24580
  2.2 16.8 %copy-start.7 = (s32[1,1,2048]{2,1,0:T(1,128)S(1)}, s32[1,1,2048]{2,1,0:T(1,128)}, u32[]{:S(2)}) copy-start(s32[1,1,2048]{2,1,0:T(1,128)} %param.9) | copy-start | bytes 24580
  2.2 16.8 %copy-start.8 = (s32[1,2]{1,0:T(1,128)S(1)}, s32[1,2]{1,0:T(1,128)}, u32[]{:S(2)}) copy-start(s32[1,2]{1,0:T(1,128)} %param.12) | copy-start | bytes 28
  17.3 1.6 %copy-start = (bf16[4,2,36,40,128]{4,3,2,1,0:T(8,128)(2,1)}, bf16[4,2,36,40,128]{4,3,2,1,0:T(8,128)(2,1)S(1)}, u32[]{:S(2)}) copy-start(bf16[4,2,36,40,128]{4,3,2,1,0:T(8,128)(2,1)S(1)} %shard_map.73.pack) | copy-start | bytes 8847364
  18.9 51.0 %copy-start.4 = (f32[36,36]{1,0:T(8,128)S(1)}, f32[36,36]{1,0:T(8,128)}, u32[]{:S(2)}) copy-start(f32[36,36]{1,0:T(8,128)} %param.8) | copy-start | bytes 15556
  69.1 74.9 %copy-start.3 = (f32[2,36,48]{2,0,1:T(2,128)S(1)}, f32[2,36,48]{2,0,1:T(2,128)}, u32[]{:S(2)}) copy-start(f32[2,36,48]{2,0,1:T(2,128)} %param.13) | copy-start | bytes 41476
  70.1 2.2 %copy-start.1 = (bf16[4,2,52,40,128]{4,3,2,1,0:T(8,128)(2,1)S(1)}, bf16[4,2,52,40,128]{4,3,2,1,0:T(8,128)(2,1)}, u32[]{:S(2)}) copy-start(bf16[4,2,52,40,128]{4,3,2,1,0:T(8,128)(2,1)} %get-tuple-element.8) | copy-start | bytes 12779524
  72.3 1.0 copy-start.2

commit v3 on v2

--- a/solution.py
+++ b/solution.py
@@ -30,7 +30,6 @@
 
     @pl.when(lax.rem(hour, hours_sec) == 0)
     def _():
-        cols_at = 4
         count = obs_ref.shape[-1]
         for piece, (begin, width, shift) in enumerate(
             ((halo, band_cols, 0), (0, halo, -band_cols), (halo + band_cols, halo, band_cols))
@@ -48,6 +47,7 @@
                 for p in range(probes)
             ]
             rhs = jnp.concatenate([x[0] for x in parts] + [x[1] for x in parts], axis=0)
+            cols_at = max(n for n in range(1, 19) if width % n == 0)
             chunk = lax.broadcasted_iota(jnp.int32, (cols_at * lev_pad, count), 0)
 
             def body(i, carry):
@@ -70,44 +70,53 @@
     @pl.when(hour > 0)
     def _():
         mix = mix_ref[...]
+        wide = 8
+        deep = 4
 
         def mixing(i, carry):
-            x = jnp.concatenate([state[2 * i], state[2 * i + 1]], axis=1)
-            low = x - x.astype(jnp.bfloat16).astype(jnp.float32)
-            stack = jnp.concatenate([x, x, low], axis=0).astype(jnp.bfloat16)
-            got = jnp.dot(mix, stack, preferred_element_type=jnp.float32)
-            mixed[2 * i] = got[:, :lanes]
-            mixed[2 * i + 1] = got[:, lanes:]
+            at = jnp.minimum(halo - hour + i * wide, ext_cols - wide)
+            for c in range(0, wide, 2):
+                x = jnp.concatenate([state[at + c], state[at + c + 1]], axis=1)
+                low = x - x.astype(jnp.bfloat16).astype(jnp.float32)
+                stack = jnp.concatenate([x, x, low], axis=0).astype(jnp.bfloat16)
+                got = jnp.dot(mix, stack, preferred_element_type=jnp.float32)
+                mixed[at + c] = got[:, :lanes]
+                mixed[at + c + 1] = got[:, lanes:]
             return carry
 
-        lax.fori_loop(0, ext_cols // 2, mixing, 0, unroll=4)
+        lax.fori_loop(0, (band_cols + 2 * hour + wide - 1) // wide, mixing, 0)
 
         lane = lax.broadcasted_iota(jnp.int32, (lev_pad, lanes), 1)
         first = lane < window
         grid_row = lax.rem(lane, window) + first_row
         keep = jnp.logical_and(grid_row >= 0, grid_row < lat_rows - 1)
 
-        def advect(j, carry):
-            packed = winds_ref[0, j].astype(jnp.float32)
-            turned = pltpu.roll(packed, window, 1)
-            before = winds_ref[0, j - 1].astype(jnp.float32)
-            east = jnp.where(first, packed, turned)
-            west = jnp.where(first, before, pltpu.roll(before, window, 1))
-            north = jnp.where(first, turned, packed)
-            north = jnp.where(keep, north, 0.0)
-            south = pltpu.roll(north, 1, 1)
-            here = mixed[j]
-            g = (
-                here
-                + jnp.maximum(east, 0.0) * (mixed[j + 1] - here)
-                + jnp.minimum(west, 0.0) * (here - mixed[j - 1])
-            )
-            above = pltpu.roll(g, lanes - 1, 1)
-            below = pltpu.roll(g, 1, 1)
-            state[j] = g + jnp.maximum(north, 0.0) * (above - g) + jnp.minimum(south, 0.0) * (g - below)
+        def advect(i, carry):
+            at = jnp.minimum(halo - hour + 1 + i * deep, ext_cols - 1 - deep)
+            packed = winds_ref[0, at - 1].astype(jnp.float32)
+            west = jnp.where(first, packed, pltpu.roll(packed, window, 1))
+            before, here = mixed[at - 1], mixed[at]
+            for c in range(deep):
+                after = mixed[at + c + 1]
+                packed = winds_ref[0, at + c].astype(jnp.float32)
+                turned = pltpu.roll(packed, window, 1)
+                east = jnp.where(first, packed, turned)
+                north = jnp.where(keep, jnp.where(first, turned, packed), 0.0)
+                south = pltpu.roll(north, 1, 1)
+                g = (
+                    here
+                    + jnp.maximum(east, 0.0) * (after - here)
+                    + jnp.minimum(west, 0.0) * (here - before)
+                )
+                above = pltpu.roll(g, lanes - 1, 1)
+                below = pltpu.roll(g, 1, 1)
+                state[at + c] = (
+                    g + jnp.maximum(north, 0.0) * (above - g) + jnp.minimum(south, 0.0) * (g - below)
+                )
+                before, here, west = here, after, east
             return carry
 
-        lax.fori_loop(1, ext_cols - 1, advect, 0, unroll=2)
+        lax.fori_loop(0, (band_cols + 2 * hour - 2 + deep - 1) // deep, advect, 0)
 
     @pl.when(step == hours - 1)
     def _():
@@ -193,67 +202,95 @@
     pl.semaphore_wait(barrier, 3 * sections)
 
     mine = pl.ds(halo + half * core, half)
-    edge = pl.ds((1 - core) * (halo + cols), halo)
     beside = lax.rem(band + bands + 2 * core - 1, bands)
-    z_copies, x_copies, h_copies, g_copies, o_copies = [], [], [], [], []
+    copies = []
     for k in range(1, sections):
         tm = lax.rem(me + k, sections)
-        z_copies.append(
+        copies.append(
             remote(
                 pack.at[tm, :, pl.ds(half * core, half)], winds.at[me, :, mine],
-                zs.at[k], zr.at[k], tm, band, core,
+                zs.at[k], zr.at[me], tm, band, core,
             )
         )
     for k in range(sections):
         tm = lax.rem(me + k, sections)
         for n, lon in enumerate(sides):
             if k or n:
-                o_copies.append(
+                copies.append(
                     remote(
-                        bundle, obs.at[me, n], os.at[3 * k + n], orr.at[3 * k + n], tm, lon, core
+                        bundle, obs.at[me, n], os.at[3 * k + n], orr.at[3 * me + n], tm, lon, core
                     )
                 )
-    x_copies.append(
-        remote(
-            pack.at[me, :, pl.ds(core * (cols - halo), halo)], winds.at[me, :, edge],
-            xs.at[0], xr.at[0], me, beside, core,
-        )
-    )
-    for k in range(1, sections):
-        source = lax.rem(me + sections - k, sections)
-        z_copies[k - 1].wait_recv()
-        h_copies.append(
-            remote(
-                winds.at[source, :, mine], winds.at[source, :, mine],
-                hs.at[k], hr.at[k], me, band, 1 - core,
-            )
-        )
-        if halo > half:
-            h_copies[-1].wait_recv()
-        x_copies.append(
-            remote(
-                winds.at[source, :, pl.ds(halo + core * (cols - halo), halo)],
-                winds.at[source, :, edge], xs.at[k], xr.at[k], me, beside, core,
-            )
-        )
-    for k in range(sections):
-        source = lax.rem(me + sections - k, sections)
-        x_copies[k].wait_recv()
-        g_copies.append(
-            remote(
-                winds.at[source, :, edge], winds.at[source, :, edge],
-                gs.at[k], gr.at[k], me, band, 1 - core,
-            )
-        )
-    if halo <= half:
-        for copy in h_copies:
-            copy.wait_recv()
-    for copy in g_copies + o_copies:
-        copy.wait_recv()
-    for copy in z_copies + x_copies + h_copies + g_copies + o_copies:
-        copy.wait_send()
     own_winds.wait()
     own_obs.wait()
+
+    def described(src, dst, send, recv, lon, probe):
+        return pltpu.make_async_remote_copy(
+            src_ref=src, dst_ref=dst, send_sem=send, recv_sem=recv,
+            device_id={"tm": me, "lon": lon, "probe": probe},
+            device_id_type=pl.DeviceIdType.MESH,
+        )
+
+    def z_copy(s):
+        place = winds.at[s, :, mine]
+        return described(place, place, zs.at[0], zr.at[s], beside, core)
+
+    def h_copy(s):
+        place = winds.at[s, :, mine]
+        return described(place, place, hs.at[s], hr.at[s], band, 1 - core)
+
+    def x_copy(s, depth):
+        src = winds.at[s, :, pl.ds(halo + core * (cols - depth), depth)]
+        dst = winds.at[s, :, pl.ds(halo - depth + (1 - core) * (cols + depth), depth)]
+        return (
+            described(src, dst, xs.at[s], xr.at[s], beside, core),
+            described(dst, dst, gs.at[s], gr.at[s], band, 1 - core),
+        )
+
+    depths = [min(halo, (s + 1) * winds.shape[1]) for s in range(sections)]
+    edges = [x_copy(s, depths[s]) for s in range(sections)]
+    order = range(sections - 1, -1, -1)
+    for s in order:
+
+        @pl.when(me == s)
+        def _():
+            edges[s][0].start()
+
+    for s in order:
+
+        @pl.when(me != s)
+        def _():
+            z_copy(s).wait_recv()
+            copy = h_copy(s)
+            copy.start()
+            if depths[s] > half:
+                copy.wait_recv()
+            edges[s][0].start()
+
+    for s in order:
+        edges[s][0].wait_recv()
+        edges[s][1].start()
+    for s in order:
+
+        @pl.when(me != s)
+        def _():
+            copy = h_copy(s)
+            if depths[s] <= half:
+                copy.wait_recv()
+            copy.wait_send()
+
+        edges[s][0].wait_send()
+        edges[s][1].wait()
+    for copy in copies:
+        copy.wait_send()
+    for k in range(sections):
+        source = lax.rem(me + k, sections)
+        for n in range(3):
+            if k or n:
+                place = obs.at[source, n]
+                described(
+                    place, place, os.at[0], orr.at[3 * source + n], beside, core
+                ).wait_recv()
 
 
 def on_device(winds, mixing, obs_cell, obs_weight, probe_sign, week_map, prior_precision):

time: 148 us -> 112 us (0.76); the launches traced: 145 us -> 111 us
  Pallas kernels: 135 us -> 101 us
    pallas_call x1, Pallas kernels: 70.7 us -> 37 us  [on_device(): pl.pallas_call(functools.partial(sweep_kernel, dims), out_shape=jax.Shape...]
where the time goes in v3:
time: 112 us; the launch traced here: 111 us
  Pallas kernels  101 us (90%)
  local copies, waits for them, and re-layouts  7.81 us (7%)
  other arithmetic  1.56 us (1%)
    pallas_call x1, Pallas kernels, on_device(): pl.pallas_call(functools.partial(spread_kernel, (sections, bands, band_co...  49.3 us
    pallas_call x1, Pallas kernels, on_device(): pl.pallas_call(functools.partial(sweep_kernel, dims), out_shape=jax.Shape...  37 us
    pallas_call x1, Pallas kernels, on_device(): pl.pallas_call(functools.partial(window_kernel, (levels, lev_pad, band_co...  15.1 us
    unnamed x20, local copies, waits for them, and re-layouts  7.09 us

profile of v3, /device:TPU:9, one launch (start us, length us, event | category | flops | bytes accessed | tf_op | source)
XLA Modules:
  0.0 110.9 jit_solution(17964107247289198922)
XLA Ops:
  0.0 2.2 %copy.13.winds_ref = bf16[2,1,2,36,36,192]{5,4,3,2,1,0:T(8,128)(2,1)S(1)} copy(bf16[2,1,2,36,36,192]{5,2,4,3,1,0:T(2,128)(2,1)} %param.7) | data formatting | bytes 3981312 | tf_op args[0]
  2.2 0.0 copy-start.5
  2.2 0.0 copy-start.6
  2.2 0.0 copy-start.7
  2.2 0.0 copy-start.8
  2.2 15.1 %shard_map.73.pack = bf16[4,2,36,40,128]{4,3,2,1,0:T(8,128)(2,1)S(1)} custom-call(bf16[2,1,2,36,36,192]{5,4,3,2,1,0:T(8,128)(2,1)S(1)} %copy.13.winds_ref), custom_call_target="tpu_custom_call" | custom-call | tf_op jit(solution)/shard_map/pallas_call | solution.py:313
  17.3 0.0 copy-start
  17.3 1.6 %copy-done = bf16[4,2,36,40,128]{4,3,2,1,0:T(8,128)(2,1)} copy-done((bf16[4,2,36,40,128]{4,3,2,1,0:T(8,128)(2,1)}, bf16[4,2,36,40,128]{4,3,2,1,0:T(8,128)(2,1)S(1)}, u32[]{:S(2)}) %copy-start) | copy-done | bytes 2949144
  18.9 0.0 copy-start.4
  18.9 0.0 copy-done.5
  18.9 0.0 copy-done.6
  18.9 0.0 copy-done.7
  19.0 0.0 copy-done.8
  19.0 0.6 select_maximum_fusion.bundle
  19.6 49.3 %shard_map.74 = (bf16[4,2,52,40,128]{4,3,2,1,0:T(8,128)(2,1)}, f32[4,3,4,2048]{3,2,1,0:T(4,128)}) custom-call(bf16[4,2,36,40,128]{4,3,2,1,0:T(8,128)(2,1)} %copy-done, f32[4,2048]{1,0:T(4,128)} %select_maximum_fusion.bundle), custom_call_target="tpu_custom_call" | custom-call | tf_op jit(solution)/shard_map/pallas_call | solution.py:336
  68.9 0.0 copy-start.3
  68.9 0.7 convert_reduce_fusion
  69.6 0.1 convert_element_type.41.weeks_ref
  69.7 0.0 copy-done.4
  69.7 0.1 copy.15
  69.8 0.1 pad_maximum_fusion.mix_ref
  69.9 0.0 copy-start.1
  69.9 2.2 %copy-done.1 = bf16[4,2,52,40,128]{4,3,2,1,0:T(8,128)(2,1)S(1)} copy-done((bf16[4,2,52,40,128]{4,3,2,1,0:T(8,128)(2,1)S(1)}, bf16[4,2,52,40,128]{4,3,2,1,0:T(8,128)(2,1)}, u32[]{:S(2)}) %copy-start.1) | copy-done | bytes 4259864
  72.1 0.0 copy-start.2
  72.1 1.0 copy-done.2
  73.1 37.0 %shard_map.75 = f32[2,36,128]{2,1,0:T(8,128)S(1)} custom-call(s32[8]{0:T(128)S(1)} %convert_element_type.41.weeks_ref, bf16[40,120]{1,0:T(8,128)(2,1)S(1)} %pad_maximum_fusion.mix_ref, bf16[8,52,40,128]{3,2,1,0:T(8,128)(2,1)S(1)} %bitcast.9, f32[4,3,4,2048]{3,2,1,0:T(4,128)S(1)} %copy-done.2), custom_call_target="tpu_custom_call" | custom-call | tf_op jit(solution)/shard_map/pallas_call | solution.py:359
  110.2 0.0 copy-done.3
  110.2 0.1 fusion
  110.3 0.6 copy.17
  (4 shorter events, 0.0 us)
Async XLA Ops:
  2.2 16.8 %copy-start.5 = (s32[2,1,1,2048]{3,2,1,0:T(1,128)S(1)}, s32[2,1,1,2048]{3,2,1,0:T(1,128)}, u32[]{:S(2)}) copy-start(s32[2,1,1,2048]{3,2,1,0:T(1,128)} %param.11) | copy-start | bytes 49156
  2.2 16.8 %copy-start.6 = (f32[1,1,2048]{2,1,0:T(1,128)S(1)}, f32[1,1,2048]{2,1,0:T(1,128)}, u32[]{:S(2)}) copy-start(f32[1,1,2048]{2,1,0:T(1,128)} %param.10) | copy-start | bytes 24580
  2.2 16.8 %copy-start.7 = (s32[1,1,2048]{2,1,0:T(1,128)S(1)}, s32[1,1,2048]{2,1,0:T(1,128)}, u32[]{:S(2)}) copy-start(s32[1,1,2048]{2,1,0:T(1,128)} %param.9) | copy-start | bytes 24580
  2.2 16.8 %copy-start.8 = (s32[1,2]{1,0:T(1,128)S(1)}, s32[1,2]{1,0:T(1,128)}, u32[]{:S(2)}) copy-start(s32[1,2]{1,0:T(1,128)} %param.12) | copy-start | bytes 28
  17.3 1.6 %copy-start = (bf16[4,2,36,40,128]{4,3,2,1,0:T(8,128)(2,1)}, bf16[4,2,36,40,128]{4,3,2,1,0:T(8,128)(2,1)S(1)}, u32[]{:S(2)}) copy-start(bf16[4,2,36,40,128]{4,3,2,1,0:T(8,128)(2,1)S(1)} %shard_map.73.pack) | copy-start | bytes 8847364
  18.9 50.8 %copy-start.4 = (f32[36,36]{1,0:T(8,128)S(1)}, f32[36,36]{1,0:T(8,128)}, u32[]{:S(2)}) copy-start(f32[36,36]{1,0:T(8,128)} %param.8) | copy-start | bytes 15556
  68.9 41.3 %copy-start.3 = (f32[2,36,48]{2,0,1:T(2,128)S(1)}, f32[2,36,48]{2,0,1:T(2,128)}, u32[]{:S(2)}) copy-start(f32[2,36,48]{2,0,1:T(2,128)} %param.13) | copy-start | bytes 41476
  69.9 2.2 %copy-start.1 = (bf16[4,2,52,40,128]{4,3,2,1,0:T(8,128)(2,1)S(1)}, bf16[4,2,52,40,128]{4,3,2,1,0:T(8,128)(2,1)}, u32[]{:S(2)}) copy-start(bf16[4,2,52,40,128]{4,3,2,1,0:T(8,128)(2,1)} %get-tuple-element.8) | copy-start | bytes 12779524
  72.1 1.0 copy-start.2

commit v4 on v3

--- a/solution.py
+++ b/solution.py
@@ -62,7 +62,10 @@
                     state[at] += add[c * lev_pad : (c + 1) * lev_pad]
                 return carry
 
-            lax.fori_loop(0, width // cols_at, body, 0)
+            trips = width // cols_at
+            if piece:
+                trips = jnp.where(hour > 0, trips, 0)
+            lax.fori_loop(0, trips, body, 0)
 
     week = weeks_ref[hour]
     flux[week] += state[halo : halo + band_cols, 0, :]
@@ -129,32 +132,42 @@
 
 
 def window_kernel(dims, winds_ref, out_ref, *tmp):
-    lev, lev_pad, cols, lat, own, left, window = dims
-    d = pl.program_id(1)
-    wide = -(-lat // 128) * 128
-    shift = lax.rem(left - d * own + 2 * wide, wide)
-    row = lax.broadcasted_iota(jnp.int32, (cols, wide), 1)
-    fill = jnp.zeros((cols, wide - lat), jnp.float32)
-
-    for part in tmp:
-        part[...] = jnp.zeros_like(part)
-
-    def level(i, carry):
-        moved = []
-        for comp in range(2):
-            x = jnp.concatenate([winds_ref[comp, 0, 0, i].astype(jnp.float32), fill], axis=1)
-            at = row - comp * window
-            at_row = at + d * own - left
-            inside = (at >= 0) & (at < window) & (at_row >= 0) & (at_row < lat)
-            turn = shift + comp * window
-            turn = jnp.where(turn >= wide, turn - wide, turn)
-            moved.append(jnp.where(inside, pltpu.roll(x, turn, 1), 0.0))
-        both = moved[0] + moved[1]
-        for n, part in enumerate(tmp):
-            part[pl.ds(i, cols, stride=lev_pad), :] = both[:, n * 128 : (n + 1) * 128]
-        return carry
-
-    lax.fori_loop(0, lev, level, 0, unroll=2)
+    sections, lev, lev_pad, cols, lat, own, left, window = dims
+    lane = lax.broadcasted_iota(jnp.int32, (cols, 128), 1)
+
+    @pl.when((pl.program_id(0) == 0) & (pl.program_id(1) == 0))
+    def _():
+        for part in tmp:
+            part[...] = jnp.zeros_like(part)
+
+    def tile(comp, i, v):
+        x = winds_ref[comp, 0, 0, i, :, v * 128 : min(v * 128 + 128, lat)].astype(jnp.float32)
+        if x.shape[1] < 128:
+            x = jnp.concatenate([x, jnp.zeros((cols, 128 - x.shape[1]), jnp.float32)], axis=1)
+        return x
+
+    def fill(start):
+        def level(i, carry):
+            for n, part in enumerate(tmp):
+                both = jnp.zeros((cols, 128), jnp.float32)
+                for comp in range(2):
+                    base = comp * window - start
+                    for v in range(-(-lat // 128)):
+                        low = max(comp * window, base + v * 128, n * 128)
+                        high = min((comp + 1) * window, base + min(v * 128 + 128, lat), n * 128 + 128)
+                        if low < high:
+                            x = tile(comp, i, v)
+                            if base % 128:
+                                x = pltpu.roll(x, base % 128, 1)
+                            inside = (lane >= low - n * 128) & (lane < high - n * 128)
+                            both = jnp.where(inside, x, both)
+                part[pl.ds(i, cols, stride=lev_pad), :] = both
+            return carry
+
+        lax.fori_loop(0, lev, level, 0, unroll=4)
+
+    for d in range(sections):
+        pl.when(pl.program_id(1) == d)(functools.partial(fill, d * own - left))
 
     def column(c, carry):
         for n, part in enumerate(tmp):
@@ -204,14 +217,17 @@
     mine = pl.ds(halo + half * core, half)
     beside = lax.rem(band + bands + 2 * core - 1, bands)
     copies = []
-    for k in range(1, sections):
-        tm = lax.rem(me + k, sections)
-        copies.append(
-            remote(
-                pack.at[tm, :, pl.ds(half * core, half)], winds.at[me, :, mine],
-                zs.at[k], zr.at[me], tm, band, core,
+    hours_sec = winds.shape[1]
+    hours = range(hours_sec - 1, -1, -1)
+    for h in hours:
+        for k in range(1, sections):
+            tm = lax.rem(me + k, sections)
+            copies.append(
+                remote(
+                    pack.at[tm, h, pl.ds(half * core, half)], winds.at[me, h, mine],
+                    zs.at[k * hours_sec + h], zr.at[me * hours_sec + h], tm, band, core,
+                )
             )
-        )
     for k in range(sections):
         tm = lax.rem(me + k, sections)
         for n, lon in enumerate(sides):
@@ -231,56 +247,60 @@
             device_id_type=pl.DeviceIdType.MESH,
         )
 
-    def z_copy(s):
-        place = winds.at[s, :, mine]
-        return described(place, place, zs.at[0], zr.at[s], beside, core)
-
-    def h_copy(s):
-        place = winds.at[s, :, mine]
-        return described(place, place, hs.at[s], hr.at[s], band, 1 - core)
-
-    def x_copy(s, depth):
-        src = winds.at[s, :, pl.ds(halo + core * (cols - depth), depth)]
-        dst = winds.at[s, :, pl.ds(halo - depth + (1 - core) * (cols + depth), depth)]
+    def z_copy(s, h):
+        place = winds.at[s, h, mine]
+        return described(place, place, zs.at[0], zr.at[s * hours_sec + h], beside, core)
+
+    def h_copy(s, h):
+        place = winds.at[s, h, mine]
+        at = s * hours_sec + h
+        return described(place, place, hs.at[at], hr.at[at], band, 1 - core)
+
+    depths = [min(halo, (s + 1) * hours_sec) for s in range(sections)]
+
+    def x_copy(s, h):
+        depth = depths[s]
+        at = s * hours_sec + h
+        src = winds.at[s, h, pl.ds(halo + core * (cols - depth), depth)]
+        dst = winds.at[s, h, pl.ds(halo - depth + (1 - core) * (cols + depth), depth)]
         return (
-            described(src, dst, xs.at[s], xr.at[s], beside, core),
-            described(dst, dst, gs.at[s], gr.at[s], band, 1 - core),
+            described(src, dst, xs.at[at], xr.at[at], beside, core),
+            described(dst, dst, gs.at[at], gr.at[at], band, 1 - core),
         )
 
-    depths = [min(halo, (s + 1) * winds.shape[1]) for s in range(sections)]
-    edges = [x_copy(s, depths[s]) for s in range(sections)]
-    order = range(sections - 1, -1, -1)
-    for s in order:
-
-        @pl.when(me == s)
+    order = [(s, h) for h in hours for s in range(sections - 1, -1, -1)]
+    edges = {at: x_copy(*at) for at in order}
+    for at in order:
+
+        @pl.when(me == at[0])
         def _():
-            edges[s][0].start()
-
-    for s in order:
-
-        @pl.when(me != s)
+            edges[at][0].start()
+
+    for at in order:
+
+        @pl.when(me != at[0])
         def _():
-            z_copy(s).wait_recv()
-            copy = h_copy(s)
+            z_copy(*at).wait_recv()
+            copy = h_copy(*at)
             copy.start()
-            if depths[s] > half:
+            if depths[at[0]] > half:
                 copy.wait_recv()
-            edges[s][0].start()
-
-    for s in order:
-        edges[s][0].wait_recv()
-        edges[s][1].start()
-    for s in order:
-
-        @pl.when(me != s)
+            edges[at][0].start()
+
+    for at in order:
+        edges[at][0].wait_recv()
+        edges[at][1].start()
+    for at in order:
+
+        @pl.when(me != at[0])
         def _():
-            copy = h_copy(s)
-            if depths[s] <= half:
+            copy = h_copy(*at)
+            if depths[at[0]] <= half:
                 copy.wait_recv()
             copy.wait_send()
 
-        edges[s][0].wait_send()
-        edges[s][1].wait()
+        edges[at][0].wait_send()
+        edges[at][1].wait()
     for copy in copies:
         copy.wait_send()
     for k in range(sections):
@@ -312,7 +332,7 @@
     shape = (hours_sec, sections, band_cols, lev_pad, 2 * window)
     pack = pl.pallas_call(
         functools.partial(
-            window_kernel, (levels, lev_pad, band_cols, lat_rows, own, left, window)
+            window_kernel, (sections, levels, lev_pad, band_cols, lat_rows, own, left, window)
         ),
         out_shape=jax.ShapeDtypeStruct((sections, hours_sec) + shape[2:], jnp.bfloat16),
         grid=(hours_sec, sections),
@@ -343,7 +363,7 @@
         ),
         in_specs=[pl.BlockSpec(memory_space=pl.ANY)] * 2,
         out_specs=(pl.BlockSpec(memory_space=pl.ANY),) * 2,
-        scratch_shapes=[sem((sections,))] * 8 + [sem((3 * sections,))] * 2 + [sem((2,))],
+        scratch_shapes=[sem((hours,))] * 8 + [sem((3 * sections,))] * 2 + [sem((2,))],
         compiler_params=pltpu.CompilerParams(collective_id=0, has_side_effects=True),
     )(pack, bundle)
     w = w.reshape((hours,) + w.shape[2:])

time: 112 us -> 104 us (0.929); the launches traced: 111 us -> 104 us
  Pallas kernels: 101 us -> 94.6 us
    pallas_call x1, Pallas kernels: 15.1 us -> 8.41 us  [on_device(): pl.pallas_call(functools.partial(window_kernel, (sections, levels, lev_pa...]
where the time goes in v4:
time: 104 us
  Pallas kernels  94.6 us (91%)
  local copies, waits for them, and re-layouts  7.81 us (8%)
  other arithmetic  1.56 us (2%)
    pallas_call x1, Pallas kernels, on_device(): pl.pallas_call(functools.partial(spread_kernel, (sections, bands, band_co...  48.2 us
    pallas_call x1, Pallas kernels, on_device(): pl.pallas_call(functools.partial(sweep_kernel, dims), out_shape=jax.Shape...  38 us
    pallas_call x1, Pallas kernels, on_device(): pl.pallas_call(functools.partial(window_kernel, (sections, levels, lev_pa...  8.41 us
    unnamed x20, local copies, waits for them, and re-layouts  7.08 us

profile of v4, /device:TPU:9, one launch (start us, length us, event | category | flops | bytes accessed | tf_op | source)
XLA Modules:
  0.0 104.1 jit_solution(9216888887467127499)
XLA Ops:
  0.0 2.2 %copy.13.winds_ref = bf16[2,1,2,36,36,192]{5,4,3,2,1,0:T(8,128)(2,1)S(1)} copy(bf16[2,1,2,36,36,192]{5,2,4,3,1,0:T(2,128)(2,1)} %param.7) | data formatting | bytes 3981312 | tf_op args[0]
  2.2 0.0 copy-start.5
  2.2 0.0 copy-start.6
  2.2 0.0 copy-start.7
  2.2 0.0 copy-start.8
  2.2 8.4 %shard_map.73.pack = bf16[4,2,36,40,128]{4,3,2,1,0:T(8,128)(2,1)S(1)} custom-call(bf16[2,1,2,36,36,192]{5,4,3,2,1,0:T(8,128)(2,1)S(1)} %copy.13.winds_ref), custom_call_target="tpu_custom_call" | custom-call | tf_op jit(solution)/shard_map/pallas_call | solution.py:333
  10.6 0.0 copy-start
  10.6 1.6 %copy-done = bf16[4,2,36,40,128]{4,3,2,1,0:T(8,128)(2,1)} copy-done((bf16[4,2,36,40,128]{4,3,2,1,0:T(8,128)(2,1)}, bf16[4,2,36,40,128]{4,3,2,1,0:T(8,128)(2,1)S(1)}, u32[]{:S(2)}) %copy-start) | copy-done | bytes 2949144
  12.2 0.0 copy-start.4
  12.2 0.0 copy-done.5
  12.2 0.0 copy-done.6
  12.3 0.0 copy-done.7
  12.3 0.0 copy-done.8
  12.3 0.6 select_maximum_fusion.bundle
  12.9 48.2 %shard_map.74 = (bf16[4,2,52,40,128]{4,3,2,1,0:T(8,128)(2,1)}, f32[4,3,4,2048]{3,2,1,0:T(4,128)}) custom-call(bf16[4,2,36,40,128]{4,3,2,1,0:T(8,128)(2,1)} %copy-done, f32[4,2048]{1,0:T(4,128)} %select_maximum_fusion.bundle), custom_call_target="tpu_custom_call" | custom-call | tf_op jit(solution)/shard_map/pallas_call | solution.py:356
  61.1 0.0 copy-start.3
  61.1 0.7 convert_reduce_fusion
  61.8 0.1 convert_element_type.41.weeks_ref
  61.9 0.0 copy-done.4
  61.9 0.1 copy.15
  62.0 0.1 pad_maximum_fusion.mix_ref
  62.1 0.0 copy-start.1
  62.1 2.2 %copy-done.1 = bf16[4,2,52,40,128]{4,3,2,1,0:T(8,128)(2,1)S(1)} copy-done((bf16[4,2,52,40,128]{4,3,2,1,0:T(8,128)(2,1)S(1)}, bf16[4,2,52,40,128]{4,3,2,1,0:T(8,128)(2,1)}, u32[]{:S(2)}) %copy-start.1) | copy-done | bytes 4259864
  64.3 0.0 copy-start.2
  64.3 1.0 copy-done.2
  65.3 38.0 %shard_map.75 = f32[2,36,128]{2,1,0:T(8,128)S(1)} custom-call(s32[8]{0:T(128)S(1)} %convert_element_type.41.weeks_ref, bf16[40,120]{1,0:T(8,128)(2,1)S(1)} %pad_maximum_fusion.mix_ref, bf16[8,52,40,128]{3,2,1,0:T(8,128)(2,1)S(1)} %bitcast.9, f32[4,3,4,2048]{3,2,1,0:T(4,128)S(1)} %copy-done.2), custom_call_target="tpu_custom_call" | custom-call | tf_op jit(solution)/shard_map/pallas_call | solution.py:379
  103.3 0.0 copy-done.3
  103.3 0.1 fusion
  103.4 0.6 copy.17
  (4 shorter events, 0.0 us)
Async XLA Ops:
  2.2 10.1 %copy-start.5 = (s32[2,1,1,2048]{3,2,1,0:T(1,128)S(1)}, s32[2,1,1,2048]{3,2,1,0:T(1,128)}, u32[]{:S(2)}) copy-start(s32[2,1,1,2048]{3,2,1,0:T(1,128)} %param.11) | copy-start | bytes 49156
  2.2 10.1 %copy-start.6 = (f32[1,1,2048]{2,1,0:T(1,128)S(1)}, f32[1,1,2048]{2,1,0:T(1,128)}, u32[]{:S(2)}) copy-start(f32[1,1,2048]{2,1,0:T(1,128)} %param.10) | copy-start | bytes 24580
  2.2 10.1 %copy-start.7 = (s32[1,1,2048]{2,1,0:T(1,128)S(1)}, s32[1,1,2048]{2,1,0:T(1,128)}, u32[]{:S(2)}) copy-start(s32[1,1,2048]{2,1,0:T(1,128)} %param.9) | copy-start | bytes 24580
  2.2 10.1 %copy-start.8 = (s32[1,2]{1,0:T(1,128)S(1)}, s32[1,2]{1,0:T(1,128)}, u32[]{:S(2)}) copy-start(s32[1,2]{1,0:T(1,128)} %param.12) | copy-start | bytes 28
  10.6 1.6 %copy-start = (bf16[4,2,36,40,128]{4,3,2,1,0:T(8,128)(2,1)}, bf16[4,2,36,40,128]{4,3,2,1,0:T(8,128)(2,1)S(1)}, u32[]{:S(2)}) copy-start(bf16[4,2,36,40,128]{4,3,2,1,0:T(8,128)(2,1)S(1)} %shard_map.73.pack) | copy-start | bytes 8847364
  12.2 49.7 %copy-start.4 = (f32[36,36]{1,0:T(8,128)S(1)}, f32[36,36]{1,0:T(8,128)}, u32[]{:S(2)}) copy-start(f32[36,36]{1,0:T(8,128)} %param.8) | copy-start | bytes 15556
  61.1 42.2 %copy-start.3 = (f32[2,36,48]{2,0,1:T(2,128)S(1)}, f32[2,36,48]{2,0,1:T(2,128)}, u32[]{:S(2)}) copy-start(f32[2,36,48]{2,0,1:T(2,128)} %param.13) | copy-start | bytes 41476
  62.1 2.2 %copy-start.1 = (bf16[4,2,52,40,128]{4,3,2,1,0:T(8,128)(2,1)S(1)}, bf16[4,2,52,40,128]{4,3,2,1,0:T(8,128)(2,1)}, u32[]{:S(2)}) copy-start(bf16[4,2,52,40,128]{4,3,2,1,0:T(8,128)(2,1)} %get-tuple-element.8) | copy-start | bytes 12779524
  64.3 1.0 copy-start.2

commit v5 on v4

--- a/solution.py
+++ b/solution.py
@@ -28,46 +28,57 @@
         mixed[...] = jnp.zeros_like(mixed)
         flux[...] = jnp.zeros_like(flux)
 
-    @pl.when(lax.rem(hour, hours_sec) == 0)
-    def _():
-        count = obs_ref.shape[-1]
+    count = obs_ref.shape[-1]
+
+    def observed(piece):
+        cell = obs_ref[0, piece, 0:1, :].astype(jnp.int32)
+        level = cell // (band_cols * lat_rows)
+        rest = cell - level * (band_cols * lat_rows)
+        column = rest // lat_rows
+        row = rest - column * lat_rows - first_row
+        hit = lax.broadcasted_iota(jnp.int32, (window, count), 0) == row
+        parts = [
+            split2(jnp.where(hit, obs_ref[0, piece, 1 + p : 2 + p, :], 0.0)) for p in range(probes)
+        ]
+        rhs = jnp.concatenate([x[0] for x in parts] + [x[1] for x in parts], axis=0)
+        return level, column, rhs
+
+    def placed_sum(hot, rhs):
+        got = lax.dot_general(
+            hot.astype(jnp.float32).astype(jnp.bfloat16), rhs, (((1,), (1,)), ((), ())),
+            preferred_element_type=jnp.float32,
+        )
+        return got[:, :lanes] + got[:, lanes:]
+
+    week = weeks_ref[hour]
+
+    @pl.when((lax.rem(hour, hours_sec) == 0) & (hour > 0))
+    def _():
         for piece, (begin, width, shift) in enumerate(
             ((halo, band_cols, 0), (0, halo, -band_cols), (halo + band_cols, halo, band_cols))
         ):
-            cell = obs_ref[0, piece, 0:1, :].astype(jnp.int32)
-            level = cell // (band_cols * lat_rows)
-            rest = cell - level * (band_cols * lat_rows)
-            column = rest // lat_rows
-            row = rest - column * lat_rows - first_row
+            level, column, rhs = observed(piece)
             place = (column + halo + shift - begin) * lev_pad + level
-            sub = lax.broadcasted_iota(jnp.int32, (window, count), 0)
-            hit = sub == row
-            parts = [
-                split2(jnp.where(hit, obs_ref[0, piece, 1 + p : 2 + p, :], 0.0))
-                for p in range(probes)
-            ]
-            rhs = jnp.concatenate([x[0] for x in parts] + [x[1] for x in parts], axis=0)
             cols_at = max(n for n in range(1, 19) if width % n == 0)
             chunk = lax.broadcasted_iota(jnp.int32, (cols_at * lev_pad, count), 0)
 
             def body(i, carry):
-                hot = (chunk == place - i * (cols_at * lev_pad)).astype(jnp.float32)
-                got = lax.dot_general(
-                    hot.astype(jnp.bfloat16), rhs, (((1,), (1,)), ((), ())),
-                    preferred_element_type=jnp.float32,
-                )
-                add = got[:, :lanes] + got[:, lanes:]
+                add = placed_sum(chunk == place - i * (cols_at * lev_pad), rhs)
                 for c in range(cols_at):
                     at = begin + i * cols_at + c
                     state[at] += add[c * lev_pad : (c + 1) * lev_pad]
                 return carry
 
-            trips = width // cols_at
-            if piece:
-                trips = jnp.where(hour > 0, trips, 0)
-            lax.fori_loop(0, trips, body, 0)
-
-    week = weeks_ref[hour]
+            lax.fori_loop(0, width // cols_at, body, 0)
+
+    @pl.when(hour == 0)
+    def _():
+        level, column, rhs = observed(0)
+        high = -(-band_cols // 8) * 8
+        chunk = lax.broadcasted_iota(jnp.int32, (high, count), 0)
+        add = placed_sum(chunk == jnp.where(level == 0, column, -1), rhs)
+        flux[week] += add[:band_cols]
+
     flux[week] += state[halo : halo + band_cols, 0, :]
 
     @pl.when(hour > 0)
@@ -344,7 +355,7 @@
         out_specs=pl.BlockSpec((1, 1) + shape[2:], lambda h, d: (d, h, 0, 0, 0)),
         scratch_shapes=[pltpu.VMEM((band_cols * lev_pad, 128), jnp.float32)]
         * (2 * window // 128),
-        compiler_params=pltpu.CompilerParams(vmem_limit_bytes=40 << 20),
+        compiler_params=pltpu.CompilerParams(vmem_limit_bytes=62 << 20),
     )(winds)
 
     value = (2 * probe_sign[:, 0, 0] - 1).astype(jnp.float32) * obs_weight[0, 0][None]
@@ -396,7 +407,7 @@
                 pltpu.VMEM((week_count, band_cols, lanes), jnp.float32),
             ],
         ),
-        compiler_params=pltpu.CompilerParams(vmem_limit_bytes=48 << 20),
+        compiler_params=pltpu.CompilerParams(vmem_limit_bytes=62 << 20),
     )(weeks, mix, w, obs)
     return (prior_precision + estimate[..., left : left + own])[None]
 

time: 104 us -> 104 us (level)
  local copies, waits for them, and re-layouts: 7.81 us -> 5.19 us
  other arithmetic: 1.56 us -> 2.94 us
    unnamed x20 -> x14, local copies, waits for them, and re-layouts: 7.08 us -> 3.87 us
    pallas_call x1, Pallas kernels: 8.41 us -> 10.9 us  [on_device(): pl.pallas_call(functools.partial(window_kernel, (sections, levels, lev_pa...]
    pallas_call x1, Pallas kernels: 38 us -> 36.3 us  [on_device(): pl.pallas_call(functools.partial(sweep_kernel, dims), out_shape=jax.Shape...]
where the time goes in v5:
time: 104 us
  Pallas kernels  95.4 us (92%)
  local copies, waits for them, and re-layouts  5.19 us (5%)
  other arithmetic  2.94 us (3%)
    pallas_call x1, Pallas kernels, on_device(): pl.pallas_call(functools.partial(spread_kernel, (sections, bands, band_co...  48.2 us
    pallas_call x1, Pallas kernels, on_device(): pl.pallas_call(functools.partial(sweep_kernel, dims), out_shape=jax.Shape...  36.3 us
    pallas_call x1, Pallas kernels, on_device(): pl.pallas_call(functools.partial(window_kernel, (sections, levels, lev_pa...  10.9 us
    unnamed x14, local copies, waits for them, and re-layouts  3.87 us

profile of v5, /device:TPU:9, one launch (start us, length us, event | category | flops | bytes accessed | tf_op | source)
XLA Modules:
  0.0 103.6 jit_solution(1982500852572863962)
XLA Ops:
  0.0 3.8 %copy.13.winds_ref = bf16[2,1,2,36,36,192]{5,4,3,2,1,0:T(8,128)(2,1)} copy(bf16[2,1,2,36,36,192]{5,2,4,3,1,0:T(2,128)(2,1)} %param.7) | data formatting | bytes 3981312 | tf_op args[0]
  3.8 0.0 copy-start.2
  3.8 0.0 copy-start.3
  3.8 0.0 copy-start.4
  3.8 0.0 copy-start.5
  3.8 10.9 %shard_map.73.pack = bf16[4,2,36,40,128]{4,3,2,1,0:T(8,128)(2,1)} custom-call(bf16[2,1,2,36,36,192]{5,4,3,2,1,0:T(8,128)(2,1)} %copy.13.winds_ref), custom_call_target="tpu_custom_call" | custom-call | tf_op jit(solution)/shard_map/pallas_call | solution.py:344
  14.7 0.0 copy-start.1
  14.7 0.0 copy-done.2
  14.7 0.0 copy-done.3
  14.7 0.0 copy-done.4
  14.8 0.0 copy-done.5
  14.8 0.6 select_maximum_fusion.bundle
  15.4 48.2 %shard_map.74 = (bf16[4,2,52,40,128]{4,3,2,1,0:T(8,128)(2,1)}, f32[4,3,4,2048]{3,2,1,0:T(4,128)}) custom-call(bf16[4,2,36,40,128]{4,3,2,1,0:T(8,128)(2,1)} %shard_map.73.pack, f32[4,2048]{1,0:T(4,128)} %select_maximum_fusion.bundle), custom_call_target="tpu_custom_call" | custom-call | tf_op jit(solution)/shard_map/pallas_call | solution.py:367
  63.6 0.0 copy-start
  63.6 0.7 convert_reduce_fusion
  64.3 0.7 convert_element_type.41.weeks_ref
  65.0 0.0 copy-done.1
  65.0 0.1 copy.15
  65.1 0.7 pad_maximum_fusion.mix_ref
  65.8 36.3 %shard_map.75 = f32[2,36,128]{2,1,0:T(8,128)} custom-call(s32[8]{0:T(128)} %convert_element_type.41.weeks_ref, bf16[40,120]{1,0:T(8,128)(2,1)} %pad_maximum_fusion.mix_ref, bf16[8,52,40,128]{3,2,1,0:T(8,128)(2,1)} %bitcast.9, f32[4,3,4,2048]{3,2,1,0:T(4,128)} %get-tuple-element.7.obs_ref), custom_call_target="tpu_custom_call" | custom-call | tf_op jit(solution)/shard_map/pallas_call | solution.py:390
  102.1 0.0 copy-done
  102.1 0.9 fusion
  103.0 0.6 copy.17
  (4 shorter events, 0.0 us)
Async XLA Ops:
  3.8 11.0 %copy-start.2 = (s32[2,1,1,2048]{3,2,1,0:T(1,128)S(1)}, s32[2,1,1,2048]{3,2,1,0:T(1,128)}, u32[]{:S(2)}) copy-start(s32[2,1,1,2048]{3,2,1,0:T(1,128)} %param.11) | copy-start | bytes 49156
  3.8 11.0 %copy-start.3 = (f32[1,1,2048]{2,1,0:T(1,128)S(1)}, f32[1,1,2048]{2,1,0:T(1,128)}, u32[]{:S(2)}) copy-start(f32[1,1,2048]{2,1,0:T(1,128)} %param.10) | copy-start | bytes 24580
  3.8 11.0 %copy-start.4 = (s32[1,1,2048]{2,1,0:T(1,128)S(1)}, s32[1,1,2048]{2,1,0:T(1,128)}, u32[]{:S(2)}) copy-start(s32[1,1,2048]{2,1,0:T(1,128)} %param.9) | copy-start | bytes 24580
  3.8 11.0 %copy-start.5 = (s32[1,2]{1,0:T(1,128)S(1)}, s32[1,2]{1,0:T(1,128)}, u32[]{:S(2)}) copy-start(s32[1,2]{1,0:T(1,128)} %param.12) | copy-start | bytes 28
  14.7 50.3 %copy-start.1 = (f32[36,36]{1,0:T(8,128)S(1)}, f32[36,36]{1,0:T(8,128)}, u32[]{:S(2)}) copy-start(f32[36,36]{1,0:T(8,128)} %param.8) | copy-start | bytes 15556
  63.6 38.5 %copy-start = (f32[2,36,48]{2,0,1:T(2,128)S(1)}, f32[2,36,48]{2,0,1:T(2,128)}, u32[]{:S(2)}) copy-start(f32[2,36,48]{2,0,1:T(2,128)} %param.13) | copy-start | bytes 41476

commit v6 on v5

--- a/solution.py
+++ b/solution.py
@@ -355,7 +355,7 @@
         out_specs=pl.BlockSpec((1, 1) + shape[2:], lambda h, d: (d, h, 0, 0, 0)),
         scratch_shapes=[pltpu.VMEM((band_cols * lev_pad, 128), jnp.float32)]
         * (2 * window // 128),
-        compiler_params=pltpu.CompilerParams(vmem_limit_bytes=62 << 20),
+        compiler_params=pltpu.CompilerParams(vmem_limit_bytes=40 << 20),
     )(winds)
 
     value = (2 * probe_sign[:, 0, 0] - 1).astype(jnp.float32) * obs_weight[0, 0][None]

time: 104 us -> 101 us (0.971)
  Pallas kernels: 95.4 us -> 92.9 us
    pallas_call x1, Pallas kernels: 10.9 us -> 8.41 us  [on_device(): pl.pallas_call(functools.partial(window_kernel, (sections, levels, lev_pa...]
    unnamed x14 -> x16, local copies, waits for them, and re-layouts: 3.87 us -> 3.89 us
where the time goes in v6:
time: 101 us
  Pallas kernels  92.9 us (92%)
  local copies, waits for them, and re-layouts  5.19 us (5%)
  other arithmetic  2.94 us (3%)
    pallas_call x1, Pallas kernels, on_device(): pl.pallas_call(functools.partial(spread_kernel, (sections, bands, band_co...  48.2 us
    pallas_call x1, Pallas kernels, on_device(): pl.pallas_call(functools.partial(sweep_kernel, dims), out_shape=jax.Shape...  36.3 us
    pallas_call x1, Pallas kernels, on_device(): pl.pallas_call(functools.partial(window_kernel, (sections, levels, lev_pa...  8.41 us
    unnamed x16, local copies, waits for them, and re-layouts  3.89 us

profile of v6, /device:TPU:9, one launch (start us, length us, event | category | flops | bytes accessed | tf_op | source)
XLA Modules:
  0.0 101.1 jit_solution(12258159717774705129)
XLA Ops:
  0.0 2.2 %copy.13.winds_ref = bf16[2,1,2,36,36,192]{5,4,3,2,1,0:T(8,128)(2,1)S(1)} copy(bf16[2,1,2,36,36,192]{5,2,4,3,1,0:T(2,128)(2,1)} %param.7) | data formatting | bytes 3981312 | tf_op args[0]
  2.2 0.0 copy-start.3
  2.2 0.0 copy-start.4
  2.2 0.0 copy-start.5
  2.2 0.0 copy-start.6
  2.2 8.4 %shard_map.73.pack = bf16[4,2,36,40,128]{4,3,2,1,0:T(8,128)(2,1)S(1)} custom-call(bf16[2,1,2,36,36,192]{5,4,3,2,1,0:T(8,128)(2,1)S(1)} %copy.13.winds_ref), custom_call_target="tpu_custom_call" | custom-call | tf_op jit(solution)/shard_map/pallas_call | solution.py:344
  10.6 0.0 copy-start
  10.6 1.6 %copy-done = bf16[4,2,36,40,128]{4,3,2,1,0:T(8,128)(2,1)} copy-done((bf16[4,2,36,40,128]{4,3,2,1,0:T(8,128)(2,1)}, bf16[4,2,36,40,128]{4,3,2,1,0:T(8,128)(2,1)S(1)}, u32[]{:S(2)}) %copy-start) | copy-done | bytes 2949144
  12.2 0.0 copy-start.2
  12.2 0.0 copy-done.3
  12.2 0.0 copy-done.4
  12.3 0.0 copy-done.5
  12.3 0.0 copy-done.6
  12.3 0.6 select_maximum_fusion.bundle
  13.0 48.2 %shard_map.74 = (bf16[4,2,52,40,128]{4,3,2,1,0:T(8,128)(2,1)}, f32[4,3,4,2048]{3,2,1,0:T(4,128)}) custom-call(bf16[4,2,36,40,128]{4,3,2,1,0:T(8,128)(2,1)} %copy-done, f32[4,2048]{1,0:T(4,128)} %select_maximum_fusion.bundle), custom_call_target="tpu_custom_call" | custom-call | tf_op jit(solution)/shard_map/pallas_call | solution.py:367
  61.1 0.0 copy-start.1
  61.1 0.7 convert_reduce_fusion
  61.9 0.7 convert_element_type.41.weeks_ref
  62.5 0.0 copy-done.2
  62.5 0.1 copy.15
  62.6 0.7 pad_maximum_fusion.mix_ref
  63.3 36.3 %shard_map.75 = f32[2,36,128]{2,1,0:T(8,128)} custom-call(s32[8]{0:T(128)} %convert_element_type.41.weeks_ref, bf16[40,120]{1,0:T(8,128)(2,1)} %pad_maximum_fusion.mix_ref, bf16[8,52,40,128]{3,2,1,0:T(8,128)(2,1)} %bitcast.9, f32[4,3,4,2048]{3,2,1,0:T(4,128)} %get-tuple-element.7.obs_ref), custom_call_target="tpu_custom_call" | custom-call | tf_op jit(solution)/shard_map/pallas_call | solution.py:390
  99.6 0.0 copy-done.1
  99.6 0.9 fusion
  100.5 0.6 copy.17
  (4 shorter events, 0.0 us)
Async XLA Ops:
  2.2 10.1 %copy-start.3 = (s32[2,1,1,2048]{3,2,1,0:T(1,128)S(1)}, s32[2,1,1,2048]{3,2,1,0:T(1,128)}, u32[]{:S(2)}) copy-start(s32[2,1,1,2048]{3,2,1,0:T(1,128)} %param.11) | copy-start | bytes 49156
  2.2 10.1 %copy-start.4 = (f32[1,1,2048]{2,1,0:T(1,128)S(1)}, f32[1,1,2048]{2,1,0:T(1,128)}, u32[]{:S(2)}) copy-start(f32[1,1,2048]{2,1,0:T(1,128)} %param.10) | copy-start | bytes 24580
  2.2 10.1 %copy-start.5 = (s32[1,1,2048]{2,1,0:T(1,128)S(1)}, s32[1,1,2048]{2,1,0:T(1,128)}, u32[]{:S(2)}) copy-start(s32[1,1,2048]{2,1,0:T(1,128)} %param.9) | copy-start | bytes 24580
  2.2 10.1 %copy-start.6 = (s32[1,2]{1,0:T(1,128)S(1)}, s32[1,2]{1,0:T(1,128)}, u32[]{:S(2)}) copy-start(s32[1,2]{1,0:T(1,128)} %param.12) | copy-start | bytes 28
  10.6 1.6 %copy-start = (bf16[4,2,36,40,128]{4,3,2,1,0:T(8,128)(2,1)}, bf16[4,2,36,40,128]{4,3,2,1,0:T(8,128)(2,1)S(1)}, u32[]{:S(2)}) copy-start(bf16[4,2,36,40,128]{4,3,2,1,0:T(8,128)(2,1)S(1)} %shard_map.73.pack) | copy-start | bytes 8847364
  12.2 50.3 %copy-start.2 = (f32[36,36]{1,0:T(8,128)S(1)}, f32[36,36]{1,0:T(8,128)}, u32[]{:S(2)}) copy-start(f32[36,36]{1,0:T(8,128)} %param.8) | copy-start | bytes 15556
  61.1 38.5 %copy-start.1 = (f32[2,36,48]{2,0,1:T(2,128)S(1)}, f32[2,36,48]{2,0,1:T(2,128)}, u32[]{:S(2)}) copy-start(f32[2,36,48]{2,0,1:T(2,128)} %param.13) | copy-start | bytes 41476
